TPU v7x, 256 devices: a whole 4x4x8 slice. The times are simulated.
256 devices in a mesh: vir: 32 (over z, y), fit: 8 (over x, core).
Axes of the slice: x: 4, y: 4, z: 8, core: 2. Of those that a mesh axis runs over, the one named last changes fastest.
Arguments:
- fitted: bfloat16 [2, 2400, 24, 7168], P(None, 'vir', None, 'fit'), may hold values from -0.0234375 to 0.0234375
- vcouple: bfloat16 [2, 2400, 2400], P(None, 'fit'), may hold values from -0.125 to 0.125
- actfock: float32 [2, 24, 24], replicated, may hold values from -1.25 to 1.25
- eps_vir: float32 [2400], P('vir'), may hold values from 0.5 to 4
- eps_act: float32 [24], replicated, may hold values from -0.5 to 0.5
- pair_energy: float32 [64], replicated, may hold values from -3 to -2
- source: float32 [2, 2400, 1536], P(None, 'vir'), may hold values from -6 to 6
Outputs:
- amplitude: float32 [2, 2400, 1536], P(None, 'vir')
All inputs are finite; a program needn't handle non-finite values.
Results may differ from a plain program's by a relative error of at most 0.0026.
Values may be sent and summed in bfloat16 or wider, within the bound.
No kernel may reach another device: no remote copies, remote signals or barrier semaphores. Data moves between devices by JAX's collectives and lax.ppermute only.
A program may use at most 128 MiB of HBM per device.

v0:
```python
import functools

import jax
import jax.numpy as jnp
from jax import lax
from jax.experimental import pallas as pl
from jax.experimental.pallas import tpu as pltpu
from jax.sharding import Mesh
from jax.sharding import PartitionSpec as P

PASSES = 3
VIR = ("z", "y")
FIT = ("x", "c")
F32 = jnp.float32
BF16 = jnp.bfloat16
LANES = 128
GROUP = 10
CHUNK = 256
STRIPS = 4
LARGE = 36 << 20
SMALL = 12 << 20


def low_count(avir):
    return -(-avir // (2 * GROUP)) * GROUP


def lane(shape):
    return lax.broadcasted_iota(jnp.int32, shape, len(shape) - 1)


def turned(both):
    ahead = pltpu.roll(both, LANES - 32, 1)
    behind = pltpu.roll(both, 32, 1)
    return jnp.where((lane(both.shape) & 32) == 0, -ahead, behind)


def merged(left, right):
    first = lane(left.shape) < 64
    return (
        jnp.where(first, left, pltpu.roll(right, 64, 1)),
        jnp.where(first, pltpu.roll(left, 64, 1), right),
    )


def mxu(left, right, dims=((1,), (0,))):
    return lax.dot_general(left, right, (dims, ((), ())), preferred_element_type=F32)


def steps_of(rows):
    return -(-rows // CHUNK)


def buffer_rows(rows):
    return rows + steps_of(rows) * CHUNK


def strips(rows, width):
    depth = 2 * rows // STRIPS
    return [[(at, min(at + depth, width))] for at in range(0, width, depth)]


def pairs_of(rows, width):
    out = []
    for at in range(0, rows, CHUNK):
        ends = ((at, min(at + CHUNK, rows)), (rows + at, min(rows + at + CHUNK, width)))
        out.append([(first, end) for first, end in ends if end > first])
    return out


def fetches(blocks, buf, sems, plan):
    width = blocks[0].shape[1]
    buf[:, :, width:, :] = jnp.zeros(
        (buf.shape[0], 2, buf.shape[2] - width, buf.shape[3]), BF16
    )
    copies = []
    for n, ranges in enumerate(plan):
        step = []
        for s, ref in enumerate(blocks):
            for k, (first, end) in enumerate(ranges):
                where = pl.ds(first, end - first)
                step.append(
                    pltpu.make_async_copy(
                        ref.at[:, where, :], buf.at[s, :, where, :], sems.at[n, s, k]
                    )
                )
        copies.append(step)
    for step in copies:
        for copy in step:
            copy.start()
    return copies


def wait_for(copies, n):
    for i, step in enumerate(copies):

        @pl.when(n == i)
        def _():
            for copy in step:
                copy.wait()


def tiles_per_row(nfit, vir_count):
    count = -(-nfit // LANES)
    while 16 * count % (2 * vir_count):
        count += 1
    return count


def set_updated(state_ref, recvs, prev_ref, kron_ref, start_ref, inv_ref, act):
    block = GROUP * act

    @pl.loop(0, start_ref.shape[0] // block, unroll=2 if start_ref.shape[0] % (2 * block) == 0 else 1)
    def _(n):
        where = pl.ds(pl.multiple_of(n * block, block), block)
        value = prev_ref[where, :]
        head = value.astype(BF16)
        tail = (value - head.astype(F32)).astype(BF16)
        both = mxu(kron_ref[...], jnp.concatenate([head, tail, head], axis=0))
        values = [recv[where, :].astype(F32) for recv in recvs]
        while len(values) > 1:
            values = [values[i] + values[i + 1] for i in range(0, len(values), 2)]
        total = both[:block] + turned(both[block:]) + values[0]
        state_ref[where, :] = start_ref[where, :] - total * inv_ref[where, :]


def set_share(state_ref, share_ref, act):
    low = state_ref.shape[0] // act
    count = share_ref.shape[0] // low
    first = lax.axis_index("x") * count
    for i in range(0, count, 2):
        both = [state_ref[pl.ds(first + i + k, low, stride=act), :] for k in range(2)]
        share_ref[i * low : (i + 2) * low, :] = jnp.concatenate(both, axis=0).astype(BF16)


def overlap(state_ref, pieces_ref, buf, acc, across, copies):
    rows = state_ref.shape[0]
    value = state_ref[...].T
    spare = jnp.zeros((64, across.shape[3] - rows), F32)
    for half in range(2):
        re = value[64 * half : 64 * half + 32]
        im = value[64 * half + 32 : 64 * half + 64]
        for k, order in enumerate(((re, im), (im, -re))):
            both = jnp.concatenate([jnp.concatenate(order, axis=0), spare], axis=1)
            across[half, k] = both.astype(BF16)
    count = buf.shape[0]
    acc[...] = jnp.zeros(acc.shape, F32)

    @pl.loop(0, len(copies))
    def _(n):
        wait_for(copies, n)
        here = pl.ds(pl.multiple_of(n * CHUNK, CHUNK), CHUNK)
        left = [[across[half, k, :, here] for k in range(2)] for half in range(2)]
        for s in range(count):
            total = None
            for half in range(2):
                there = pl.ds(pl.multiple_of(half * rows + n * CHUNK, 16), CHUNK)
                for k in range(2):
                    term = mxu(left[half][k], buf[s, k, there, :])
                    total = term if total is None else total + term
            acc[s] += total

    sums = [acc[s] for s in range(count)]
    nfit = sums[0].shape[1]
    pieces, depth, _ = pieces_ref.shape
    groups = 8 * count
    wide = pieces * depth // (8 * groups)

    def tile(slot):
        group, k = divmod(slot, wide)
        if k * LANES >= nfit:
            return jnp.zeros((8, LANES), F32)
        s, at = divmod(group * 8, 64)
        return sums[s][at : at + 8, k * LANES : (k + 1) * LANES]

    for slot in range(0, groups * wide, 2):
        both = jnp.concatenate([tile(slot), tile(slot + 1)], axis=0).astype(BF16)
        piece, at = divmod(slot * 8, depth)
        pieces_ref[piece, at : at + 16, :] = both


def spread(pieces_ref, outs):
    me = lax.axis_index("y")
    for k, out in enumerate(outs):
        out[...] = pieces_ref[me ^ k]


def prepare(source_ref, vir_ref, act_ref, pair_ref, start_ref, inv_ref, act):
    core = lax.axis_index("c")
    avir = source_ref.shape[1]
    low = start_ref.shape[0] // act
    spare = 2 * low - avir
    at = lane((low, LANES))
    row = lax.broadcasted_iota(jnp.int32, (low, LANES), 0)
    held = (at < 64) | (row < low - spare)

    def lifted(values, fill):
        rest = jnp.full((spare, values.shape[1]), fill, F32)
        return values[:low], jnp.concatenate([values[low:], rest], axis=0)

    above = lifted(jnp.broadcast_to(vir_ref[...], (avir, LANES)), 1.0)
    above = jnp.where(at < 64, above[0], above[1]) - pair_ref[...]

    @pl.loop(0, act // 2, unroll=3)
    def _(pair):
        sides = []
        for part in range(2):
            where = pl.ds(pl.multiple_of(pair * LANES, LANES), LANES)
            values = source_ref[part, :, where]
            values = jnp.where(core == 0, values, pltpu.roll(values, LANES - 32, 1))
            sides += lifted(values, 0.0)
        order = (sides[0], sides[2], sides[1], sides[3])
        for k in range(2):
            t = 2 * pair + k
            value = None
            for n in (3, 2, 1, 0):
                shift = (32 * n - 64 * k) % LANES
                moved = pltpu.roll(order[n], shift, 1) if shift else order[n]
                value = moved if value is None else jnp.where(at < 32 * (n + 1), moved, value)
            inverse = jnp.where(held, 1.0 / (above + act_ref[t]), 0.0)
            inv_ref[pl.ds(t, low, stride=act), :] = inverse
            start_ref[pl.ds(t, low, stride=act), :] = value * inverse


def opening_kernel(
    act, source_ref, vir_ref, act_ref, pair_ref, own,
    start_ref, inv_ref, share_ref, pieces_ref, *scratch,
):
    buf, sems, acc, across = scratch
    copies = fetches([own], buf, sems, pairs_of(start_ref.shape[0], own.shape[1]))
    prepare(source_ref, vir_ref, act_ref, pair_ref, start_ref, inv_ref, act)
    set_share(start_ref, share_ref, act)
    overlap(start_ref, pieces_ref, buf, acc, across, copies)


def second_kernel(start_ref, first_ref, other, *rest):
    *outs, pieces, buf, sems, acc, across = rest
    copies = fetches([other], buf, sems, pairs_of(start_ref.shape[0], other.shape[1]))
    count = first_ref.shape[0]
    pieces[:count] = first_ref[...]
    overlap(start_ref, pieces.at[count:], buf, acc, across, copies)
    spread(pieces, outs)


def next_kernel(act, nx, *refs):
    prev_ref, kron_ref, start_ref, inv_ref, own, other, state_ref, share_ref, *rest = refs[nx:]
    *outs, pieces, buf, sems, acc, across = rest
    copies = fetches([own, other], buf, sems, pairs_of(start_ref.shape[0], own.shape[1]))
    set_updated(state_ref, refs[:nx], prev_ref, kron_ref, start_ref, inv_ref, act)
    set_share(state_ref, share_ref, act)
    overlap(state_ref, pieces, buf, acc, across, copies)
    spread(pieces, outs)


def last_kernel(act, nx, *refs):
    prev_ref, kron_ref, start_ref, inv_ref, state_ref = refs[nx:]
    set_updated(state_ref, refs[:nx], prev_ref, kron_ref, start_ref, inv_ref, act)


def kron_kernel(fock_ref, out_ref):
    act = fock_ref.shape[1]
    block = GROUP * act
    row = lax.broadcasted_iota(jnp.int32, (block, act), 0)
    col = lax.broadcasted_iota(jnp.int32, (block, act), 1)
    pick = jnp.where(lax.rem(row, act) == col, 1.0, 0.0).astype(BF16)
    row = lax.broadcasted_iota(jnp.int32, (block, block), 0)
    col = lax.broadcasted_iota(jnp.int32, (block, block), 1)
    same = lax.div(row, act) == lax.div(col, act)
    last = ((1,), (1,))
    for part in range(2):
        value = fock_ref[part]
        head = value.astype(BF16)
        rest = (value - head.astype(F32)).astype(BF16)
        tables = []
        for term in (head, rest):
            table = mxu(mxu(pick, term, last).astype(BF16), pick, last)
            tables.append(jnp.where(same, table, 0.0))
        out_ref[part * block : (part + 1) * block, :] = jnp.concatenate(
            [tables[0], tables[0], tables[1]], axis=1
        ).astype(BF16)


def output_kernel(act, mine_ref, theirs_ref, out_ref):
    core = lax.axis_index("c")
    avir = out_ref.shape[1]
    low = mine_ref.shape[0] // act
    at = lane((low, LANES))

    @pl.loop(0, act // 2, unroll=3)
    def _(pair):
        order = []
        for k in range(2):
            where = pl.ds(2 * pair + k, low, stride=act)
            mine, theirs = mine_ref[where, :], theirs_ref[where, :]
            order.append(jnp.where(core == 0, mine, theirs))
            order.append(jnp.where(core == 0, theirs, mine))
        for side in range(2):
            for part in range(2):
                value = None
                for n in (3, 2, 1, 0):
                    shift = (32 * n - 64 * side - 32 * part) % LANES
                    moved = pltpu.roll(order[n], shift, 1) if shift else order[n]
                    value = moved if value is None else jnp.where(at < 32 * (n + 1), moved, value)
                rows = low if side == 0 else avir - low
                where = pl.ds(pl.multiple_of(pair * LANES, LANES), LANES)
                out_ref[part, pl.ds(side * low, rows), where] = value[:rows]


def total_of(refs, at, rows):
    total = refs[0][at : at + rows, :].astype(F32)
    for ref in refs[1:]:
        total += ref[at : at + rows, :].astype(F32)
    return total


def along_z_kernel(*refs):
    *recvs, share_ref, out_ref = refs
    nz, rows, _ = out_ref.shape
    depth = rows - share_ref.shape[0]
    share = share_ref[...]
    for z in range(nz):
        out_ref[z, :depth, :] = total_of(recvs, z * depth, depth).astype(BF16)
        out_ref[z, depth:, :] = share


def sum_kernel(recv_ref, out_ref):
    nz, rows, _ = out_ref.shape
    total = total_of([recv_ref.at[z] for z in range(nz)], 0, rows).astype(BF16)
    for i in range(nz):
        out_ref[i] = total


def couple_kernel(recv_ref, couple_ref, out_ref):
    nz, height, _ = recv_ref.shape
    ny, rows, _ = out_ref.shape
    low = couple_ref.shape[1] // (2 * nz)
    base = height - rows
    couple = couple_ref[...]
    half = couple.shape[0] // 2

    @pl.loop(0, rows // (2 * low))
    def _(n):
        at = pl.multiple_of(n * 2 * low, 16)
        lines = []
        for z in range(nz):
            there = pl.ds(pl.multiple_of(base + n * 2 * low, 16), 2 * low)
            both = recv_ref[z, there, :].astype(F32)
            lines += merged(both[:low], both[low:])
        both = mxu(couple, jnp.concatenate(lines, axis=0).astype(BF16))
        term = both[:half] + turned(both[half:])
        for y in range(ny):
            top = y * 2 * low
            pieces = merged(term[top : top + low], term[top + low : top + 2 * low])
            out_ref[y, pl.ds(at, 2 * low), :] = jnp.concatenate(pieces, axis=0).astype(BF16)


def along_y_kernel(inter_ref, vir_ref, *outs):
    nz, depth, _ = inter_ref.shape
    me = lax.axis_index("y")
    for k, out in enumerate(outs):
        for z in range(nz):
            out[z * depth : (z + 1) * depth, :] = inter_ref[z]
        out[nz * depth :, :] = vir_ref[me ^ k]


def tail_kernel(act, height, *refs):
    *recvs, own, other, out_ref, inter_ref, both, total, right, recv_sems, buf, sems = refs
    rows = out_ref.shape[0]
    nfit = own.shape[2]
    me = lax.axis_index("y")
    moves = [
        pltpu.make_async_copy(recv, inter_ref.at[me ^ k], recv_sems.at[k])
        for k, recv in enumerate(recvs)
    ]
    for move in moves:
        move.start()
    copies = fetches([own, other], buf, sems, strips(rows, own.shape[1]))
    for move in moves:
        move.wait()
    wide = inter_ref.shape[0] * height // LANES
    tiles = {}
    for slot in range(0, 16 * wide, 2):
        piece, at = divmod(slot * 8, height)
        pair = inter_ref[piece, at : at + 16, :].astype(F32)
        tiles[slot], tiles[slot + 1] = pair[:8], pair[8:]
    count = -(-nfit // LANES)
    lines = [
        jnp.concatenate([tiles[g * wide + k] for k in range(count)], axis=1)
        for g in range(16)
    ]
    for s in range(2):
        re = jnp.concatenate(lines[8 * s : 8 * s + 4], axis=0)
        im = jnp.concatenate(lines[8 * s + 4 : 8 * s + 8], axis=0)
        for k, order in enumerate(((re, im), (-im, re))):
            right[s, k] = jnp.concatenate([*order, *order], axis=0).astype(BF16)

    depth = 2 * rows // STRIPS

    @pl.loop(0, len(copies))
    def _(n):
        wait_for(copies, n)
        there = pl.ds(pl.multiple_of(n * depth, 16), depth)
        here = None
        for s in range(2):
            for k in range(2):
                term = mxu(buf[s, k, there, :], right[s, k], ((1,), (1,)))
                here = term if here is None else here + term
        both[there, :] = here

    first_half = lane((rows, LANES)) < 64
    total[...] = jnp.where(first_half, both[:rows, :], both[rows:, :])
    low = rows // act
    share = (inter_ref.shape[1] - height) // low
    held = [inter_ref.at[y] for y in range(inter_ref.shape[0])]
    first = lax.axis_index("x") * share
    for i in range(0, share, 2):
        pair = total_of(held, height + i * low, 2 * low)
        for k in range(2):
            where = pl.ds(first + i + k, low, stride=act)
            total[where, :] = total[where, :] + pair[k * low : (k + 1) * low]
    out_ref[...] = total[...].astype(BF16)


VMEM = pl.BlockSpec(memory_space=pltpu.VMEM)
HBM = pl.BlockSpec(memory_space=pltpu.HBM)
SMEM = pl.BlockSpec(memory_space=pltpu.SMEM)


def call(body, outs, ins, scratch=(), name=None, flops=0, moved=0):
    return pl.pallas_call(
        body,
        out_shape=outs,
        in_specs=ins,
        out_specs=jax.tree.map(lambda _: VMEM, outs),
        scratch_shapes=scratch,
        compiler_params=pltpu.CompilerParams(vmem_limit_bytes=LARGE if flops else SMALL),
        cost_estimate=pl.CostEstimate(flops=flops, bytes_accessed=moved, transcendentals=0),
        name=name,
    )


def exchange(copies, axis):
    return lax.all_to_all(copies, axis, 0, 0, tiled=True)


def swapped(values, axis):
    size = len(values)
    return [values[0]] + [
        lax.ppermute(values[k], axis, [(i, i ^ k) for i in range(size)]) for k in range(1, size)
    ]


def laid_out(couple, low, ny):
    nz, _, avir, _ = couple.shape
    couple = couple.reshape(nz, 2, avir, ny, avir)
    fill = (0, 2 * low - avir)
    couple = jnp.pad(couple, ((0, 0), (0, 0), fill, (0, 0), fill))
    return couple.transpose(1, 3, 4, 0, 2).reshape(4 * ny * low, 2 * nz * low)


def per_device(fitted, vcouple, actfock, eps_vir, eps_act, pair_energy, source):
    cores, nx, ny, nz = (lax.axis_size(n) for n in ("c", "x", "y", "z"))
    core = lax.axis_index("c")
    _, avir, act, nfit = fitted.shape
    pairs = pair_energy.shape[0]
    half = pairs // cores
    width = avir * act
    low = low_count(avir)
    rows = low * act
    share = act // nx
    swap = [(0, 1), (1, 0)]
    own = fitted.reshape(2, width, nfit)
    other = lax.ppermute(own, "c", swap)

    mine = lax.dynamic_slice_in_dim(vcouple, lax.axis_index("y") * avir, avir, 1)
    mine = lax.dynamic_slice_in_dim(mine, lax.axis_index("z") * avir * ny, avir * ny, 2)
    couple = exchange(jnp.broadcast_to(mine[None], (nz, *mine.shape)), FIT)

    energy = lax.dynamic_slice_in_dim(pair_energy, core * half, half, 0)
    energy = jnp.tile(energy, LANES // half).reshape(1, LANES)

    wide = tiles_per_row(nfit, ny * nz)
    height = 16 * wide * 8 // ny
    depth = height // nz
    extra = share * low

    def sent(*shape):
        return jax.ShapeDtypeStruct((*shape, LANES), BF16)

    state_shape = jax.ShapeDtypeStruct((rows, LANES), F32)
    piece_shape, share_shape = [sent(height)] * ny, sent(extra)
    pieces = pltpu.VMEM((ny, height, LANES), BF16)
    steps = steps_of(rows)

    def fetch(count):
        return [
            pltpu.VMEM((count, 2, buffer_rows(rows), nfit), BF16),
            pltpu.SemaphoreType.DMA((max(steps, STRIPS), count, 2)),
        ]

    def sums(count):
        return fetch(count) + [
            pltpu.VMEM((count, 64, nfit), F32), pltpu.VMEM((2, 2, 64, steps * CHUNK), BF16)
        ]

    flops = 16 * width * nfit * 32
    moved = 8 * width * nfit
    opening = call(
        functools.partial(opening_kernel, act),
        [state_shape, state_shape, share_shape, sent(ny // 2, height)],
        [VMEM, VMEM, SMEM, VMEM, HBM], sums(1), "opening", flops // 2, moved // 2,
    )
    second = call(
        second_kernel, piece_shape, [VMEM, VMEM, HBM], [pieces] + sums(1), "second",
        flops // 2, moved // 2,
    )
    later = call(
        functools.partial(next_kernel, act, nx), [state_shape, share_shape] + piece_shape,
        [VMEM] * (nx + 4) + [HBM] * 2, [pieces] + sums(2), "later", flops, moved,
    )
    last = call(
        functools.partial(last_kernel, act, nx), state_shape, [VMEM] * (nx + 4), (), "last"
    )
    block = GROUP * act
    kron = call(
        kron_kernel, jax.ShapeDtypeStruct((2 * block, 3 * block), BF16), [VMEM], (), "kron"
    )(actfock)
    along_z = call(
        along_z_kernel, sent(nz, depth + extra), [VMEM] * (ny + 1), (), "along_z"
    )
    summed = call(sum_kernel, sent(nz, depth), [VMEM], (), "summed")
    coupled = call(couple_kernel, sent(ny, extra), [VMEM] * 2, (), "coupled")
    along_y = call(
        along_y_kernel, [sent(height + extra)] * ny, [VMEM] * 2, (), "along_y"
    )
    tail = call(
        functools.partial(tail_kernel, act, height), sent(rows),
        [HBM] * (ny + 2),
        [
            pltpu.VMEM((ny, height + extra, LANES), BF16),
            pltpu.VMEM((2 * rows, LANES), F32),
            pltpu.VMEM((rows, LANES), F32),
            pltpu.VMEM((2, 2, LANES, nfit), BF16),
            pltpu.SemaphoreType.DMA((ny,)),
        ]
        + fetch(2),
        "tail", flops, moved,
    )
    output = call(
        functools.partial(output_kernel, act),
        jax.ShapeDtypeStruct((2, avir, act * pairs), F32), [VMEM] * 2, (), "output",
    )

    for step in range(PASSES):
        if step == 0:
            start, inverse, share_now, part = opening(
                source, eps_vir.reshape(avir, 1), eps_act, energy, own
            )
            state = start
            part = second(start, part, other)
            part, couple = lax.optimization_barrier((part, couple))
            couple = laid_out(couple, low, ny)
        else:
            state, share_now, *part = later(*recv, state, kron, start, inverse, own, other)
        mixed = exchange(along_z(*swapped(part, "y"), share_now), "z")
        inter = exchange(summed(mixed), "z")
        mixed = swapped(along_y(inter, coupled(mixed, couple)), "y")
        recv = swapped([tail(*mixed, own, other)] * nx, "x")
    state = last(*recv, state, kron, start, inverse)
    return output(state, lax.ppermute(state, "c", swap))


def solution(mesh, sizes=(8, 4, 4, 2)):
    in_specs = (
        P(None, VIR, None, FIT),
        P(None, FIT, None),
        P(),
        P(VIR),
        P(),
        P(),
        P(None, VIR, None),
    )
    return jax.shard_map(
        per_device,
        mesh=Mesh(mesh.devices.reshape(*sizes), ("z", "y", "x", "c")),
        in_specs=in_specs,
        out_specs=P(None, VIR, None),
        check_vma=False,
    )
```

profile of v0, /device:TPU:1, one launch (start us, length us, event | category | flops | bytes accessed | tf_op | source)
XLA Modules:
  0.0 285.7 jit_solution(6428490540367030498)
XLA Ops:
  0.0 3.3 %collective-permute-start = (bf16[2,1800,896]{2,1,0:T(8,128)(2,1)}, bf16[2,1800,896]{2,1,0:T(8,128)(2,1)}, u32[]{:S(2)}, u32[]{:S(2)}) collective-permute-start(bf16[2,1800,896]{2,1,0:T(8,128)(2,1)} %bitcast.7), channel_id=1, source_target_pairs={{0,1},{1,0},{2,3},{3,2},{4,5},{5,4},{6,7},{7,6},{8,9},{9,8},{10,11... | collective-permute-start | bytes 19353608 | tf_op jit(solution)/shard_map/ppermute | solution.py:473
  5.0 5.8 %all-to-all-start = ((bf16[8,2,75,300]{3,1,2,0:T(2,128)(2,1)}), bf16[8,2,75,300]{3,1,2,0:T(2,128)(2,1)}, u32[]{:S(2)}, u32[]{:S(2)}) async-start(bf16[8,2,75,300]{3,1,2,0:T(2,128)(2,1)} %broadcast_in_dim.2), calls=%async_computation | async-start | bytes 1843200 | tf_op jit(solution)/shard_map/all_to_all | solution.py:443
  17.5 5.0 %opening.1 = (f32[960,128]{1,0:T(8,128)S(1)}, f32[960,128]{1,0:T(8,128)S(1)}, bf16[240,128]{1,0:T(8,128)(2,1)S(1)}, bf16[2,256,128]{2,1,0:T(8,128)(2,1)S(1)}) custom-call(f32[2,75,1536]{2,1,0:T(8,128)S(1)} %copy-done.19, f32[75,1]{1,0:T(8,128)S(1)} %copy.13.vir_ref, f32[24]{0:T(128)S(1)} %copy-done.32, f32[1,128]{1,0:T(1,128)S(1)} %reshape_tile.3.pair_ref, ...), custom_call_target="tpu_custom_call" | custom-call | flops 412876800 | bytes 6451200 | tf_op jit(solution)/shard_map/opening/pallas_call | solution.py:556
  23.3 3.6 %second.1 = (bf16[256,128]{1,0:T(8,128)(2,1)S(1)}, bf16[256,128]{1,0:T(8,128)(2,1)S(1)}, bf16[256,128]{1,0:T(8,128)(2,1)S(1)}, bf16[256,128]{1,0:T(8,128)(2,1)S(1)}) custom-call(f32[960,128]{1,0:T(8,128)S(1)} %get-tuple-element.42.start_ref.refs_4_.refs_6_, bf16[2,256,128]{2,1,0:T(8,128)(2,1)S(1)} %get-tuple-element.43.first_ref, ...), custom_call_target="tpu_custom_call" | custom-call | flops 412876800 | bytes 6451200 | tf_op jit(solution)/shard_map/second/pallas_call | solution.py:560
  36.8 8.2 %all-to-all-start.1 = ((bf16[8,272,128]{2,1,0:T(8,128)(2,1)}), bf16[8,272,128]{2,1,0:T(8,128)(2,1)}, u32[]{:S(2)}, u32[]{:S(2)}) async-start(bf16[8,272,128]{2,1,0:T(8,128)(2,1)} %copy-done.20), calls=%async_computation.1 | async-start | bytes 1114112 | tf_op jit(solution)/shard_map/all_to_all | solution.py:443
  44.9 3.4 %copy.16 = bf16[8,2,75,300]{2,0,3,1:T(8,128)(2,1)} copy(bf16[8,2,75,300]{3,1,2,0:T(2,128)(2,1)} %all-to-all-done) | data formatting | bytes 1440000 | tf_op jit(solution)/shard_map/reshape | solution.py:455
  48.3 13.3 %all-to-all-done.1.recv_ref = bf16[8,272,128]{2,1,0:T(8,128)(2,1)} async-done(((bf16[8,272,128]{2,1,0:T(8,128)(2,1)}), bf16[8,272,128]{2,1,0:T(8,128)(2,1)}, u32[]{:S(2)}, u32[]{:S(2)}) %all-to-all-start.1) | async-done | bytes 557088 | tf_op jit(solution)/shard_map/all_to_all | solution.py:443
  63.3 3.3 %all-to-all-start.2 = ((bf16[8,32,128]{2,1,0:T(8,128)(2,1)}), bf16[8,32,128]{2,1,0:T(8,128)(2,1)S(1)}, u32[]{:S(2)}, u32[]{:S(2)}) async-start(bf16[8,32,128]{2,1,0:T(8,128)(2,1)} %summed.3), calls=%async_computation.2 | async-start | bytes 131072 | tf_op jit(solution)/shard_map/all_to_all | solution.py:443
  83.3 5.7 %collective-permute-done.5.refs_2_ = bf16[496,128]{1,0:T(8,128)(2,1)S(1)} collective-permute-done((bf16[496,128]{1,0:T(8,128)(2,1)S(1)}, bf16[496,128]{1,0:T(8,128)(2,1)S(1)}, u32[]{:S(2)}, u32[]{:S(2)}) %collective-permute-start.5) | collective-permute-done | bytes 127008 | tf_op jit(solution)/shard_map/ppermute | solution.py:449
  94.4 7.0 %tail.3.refs_0_ = bf16[960,128]{1,0:T(8,128)(2,1)S(1)} custom-call(bf16[496,128]{1,0:T(8,128)(2,1)S(1)} %get-tuple-element.54.refs_0_, bf16[496,128]{1,0:T(8,128)(2,1)S(1)} %collective-permute-done.4.refs_1_, bf16[496,128]{1,0:T(8,128)(2,1)S(1)} %collective-permute-done.5.refs_2_, bf16[496,128]{1,0:T(8,128)(2,1)S(1)} %collective-permute-done.6.refs_3_, ...), custom_call_target="tpu_custom_call" | custom-call | flops 825753600 | bytes 12902400 | tf_op jit(solution)/shard_map/tail/pallas_call | solution.py:568
  107.8 7.1 %collective-permute-done.8.refs_2_ = bf16[960,128]{1,0:T(8,128)(2,1)S(1)} collective-permute-done((bf16[960,128]{1,0:T(8,128)(2,1)S(1)}, bf16[960,128]{1,0:T(8,128)(2,1)S(1)}, u32[]{:S(2)}, u32[]{:S(2)}) %collective-permute-start.8) | collective-permute-done | bytes 245792 | tf_op jit(solution)/shard_map/ppermute | solution.py:449
  117.6 5.9 %later.2 = (f32[960,128]{1,0:T(8,128)S(1)}, bf16[240,128]{1,0:T(8,128)(2,1)S(1)}, bf16[256,128]{1,0:T(8,128)(2,1)S(1)}, bf16[256,128]{1,0:T(8,128)(2,1)S(1)}, bf...) custom-call(bf16[960,128]{1,0:T(8,128)(2,1)S(1)} %tail.3.refs_0_, ...), custom_call_target="tpu_custom_call" | custom-call | flops 825753600 | bytes 12902400 | tf_op jit(solution)/shard_map/later/pallas_call | solution.py:564
  124.0 3.4 %collective-permute-start.12 = (bf16[256,128]{1,0:T(8,128)(2,1)S(1)}, bf16[256,128]{1,0:T(8,128)(2,1)S(1)}, u32[]{:S(2)}, u32[]{:S(2)}) collective-permute-start(bf16[256,128]{1,0:T(8,128)(2,1)S(1)} %get-tuple-element.62), channel_id=1, source_target_pairs={{0,24},{8,16},{16,8},{24,0},{1,25},{9,17},{17,9},{25,1},{2,26},{10... | collective-permute-start | bytes 196616 | tf_op jit(solution)/shard_map/ppermute | solution.py:449
  129.5 19.6 %all_to_all.35.recv_ref = bf16[8,272,128]{2,1,0:T(8,128)(2,1)S(1)} all-to-all(bf16[8,272,128]{2,1,0:T(8,128)(2,1)S(1)} %along_z.4), channel_id=1, replica_groups=mesh['z'=8,'y'=4,'x'=4,'c'=2] {'z'}, dimensions={0} | all-to-all | bytes 1114112 | tf_op jit(solution)/shard_map/all_to_all | solution.py:443
  150.6 4.4 %all-to-all-start.4 = ((bf16[8,32,128]{2,1,0:T(8,128)(2,1)}), bf16[8,32,128]{2,1,0:T(8,128)(2,1)S(1)}, u32[]{:S(2)}, u32[]{:S(2)}) async-start(bf16[8,32,128]{2,1,0:T(8,128)(2,1)} %summed.4), calls=%async_computation.4 | async-start | bytes 131072 | tf_op jit(solution)/shard_map/all_to_all | solution.py:443
  163.3 4.3 %collective-permute-start.14 = (bf16[496,128]{1,0:T(8,128)(2,1)S(1)}, bf16[496,128]{1,0:T(8,128)(2,1)S(1)}, u32[]{:S(2)}, u32[]{:S(2)}) collective-permute-start(bf16[496,128]{1,0:T(8,128)(2,1)S(1)} %get-tuple-element.66), channel_id=1, source_target_pairs={{0,16},{8,24},{16,0},{24,8},{1,17},{9,25},{17,1},{25,9},{2,18},{10... | collective-permute-start | bytes 380936 | tf_op jit(solution)/shard_map/ppermute | solution.py:449
  167.5 3.7 %collective-permute-done.14.refs_2_ = bf16[496,128]{1,0:T(8,128)(2,1)S(1)} collective-permute-done((bf16[496,128]{1,0:T(8,128)(2,1)S(1)}, bf16[496,128]{1,0:T(8,128)(2,1)S(1)}, u32[]{:S(2)}, u32[]{:S(2)}) %collective-permute-start.14) | collective-permute-done | bytes 127008 | tf_op jit(solution)/shard_map/ppermute | solution.py:449
  175.4 7.0 %tail.4.refs_0_ = bf16[960,128]{1,0:T(8,128)(2,1)S(1)} custom-call(bf16[496,128]{1,0:T(8,128)(2,1)S(1)} %get-tuple-element.64.refs_0_, bf16[496,128]{1,0:T(8,128)(2,1)S(1)} %collective-permute-done.13.refs_1_, bf16[496,128]{1,0:T(8,128)(2,1)S(1)} %collective-permute-done.14.refs_2_, bf16[496,128]{1,0:T(8,128)(2,1)S(1)} %collective-permute-done.15.refs_3_, ...), custom_call_target="tpu_custom_call" | custom-call | flops 825753600 | bytes 12902400 | tf_op jit(solution)/shard_map/tail/pallas_call | solution.py:568
  193.1 5.9 %later.3 = (f32[960,128]{1,0:T(8,128)S(1)}, bf16[240,128]{1,0:T(8,128)(2,1)S(1)}, bf16[256,128]{1,0:T(8,128)(2,1)S(1)}, bf16[256,128]{1,0:T(8,128)(2,1)S(1)}, bf...) custom-call(bf16[960,128]{1,0:T(8,128)(2,1)S(1)} %tail.4.refs_0_, ...), custom_call_target="tpu_custom_call" | custom-call | flops 825753600 | bytes 12902400 | tf_op jit(solution)/shard_map/later/pallas_call | solution.py:564
  205.2 16.6 %all_to_all.36.recv_ref = bf16[8,272,128]{2,1,0:T(8,128)(2,1)S(1)} all-to-all(bf16[8,272,128]{2,1,0:T(8,128)(2,1)S(1)} %along_z.5), channel_id=1, replica_groups=mesh['z'=8,'y'=4,'x'=4,'c'=2] {'z'}, dimensions={0} | all-to-all | bytes 1114112 | tf_op jit(solution)/shard_map/all_to_all | solution.py:443
  223.4 3.3 %all-to-all-start.6 = ((bf16[8,32,128]{2,1,0:T(8,128)(2,1)}), bf16[8,32,128]{2,1,0:T(8,128)(2,1)S(1)}, u32[]{:S(2)}, u32[]{:S(2)}) async-start(bf16[8,32,128]{2,1,0:T(8,128)(2,1)} %summed.5), calls=%async_computation.6 | async-start | bytes 131072 | tf_op jit(solution)/shard_map/all_to_all | solution.py:443
  246.4 7.0 %tail.5.refs_0_ = bf16[960,128]{1,0:T(8,128)(2,1)S(1)} custom-call(bf16[496,128]{1,0:T(8,128)(2,1)S(1)} %get-tuple-element.74.refs_0_, bf16[496,128]{1,0:T(8,128)(2,1)S(1)} %collective-permute-done.22.refs_1_, bf16[496,128]{1,0:T(8,128)(2,1)S(1)} %collective-permute-done.23.refs_2_, bf16[496,128]{1,0:T(8,128)(2,1)S(1)} %collective-permute-done.24.refs_3_, ...), custom_call_target="tpu_custom_call" | custom-call | flops 825753600 | bytes 12902400 | tf_op jit(solution)/shard_map/tail/pallas_call | solution.py:568
  258.6 4.5 %collective-permute-done.26.refs_2_ = bf16[960,128]{1,0:T(8,128)(2,1)S(1)} collective-permute-done((bf16[960,128]{1,0:T(8,128)(2,1)S(1)}, bf16[960,128]{1,0:T(8,128)(2,1)S(1)}, u32[]{:S(2)}, u32[]{:S(2)}) %collective-permute-start.26) | collective-permute-done | bytes 245792 | tf_op jit(solution)/shard_map/ppermute | solution.py:449
  267.1 14.5 %collective-permute-start.28 = (f32[960,128]{1,0:T(8,128)S(1)}, f32[960,128]{1,0:T(8,128)S(1)}, u32[]{:S(2)}, u32[]{:S(2)}) collective-permute-start(f32[960,128]{1,0:T(8,128)S(1)} %last.1.mine_ref), channel_id=1, source_target_pairs={{0,1},{1,0},{2,3},{3,2},{4,5},{5,4},{6,7},{7,6},{8,9},{9,8},{10,11... | collective-permute-start | bytes 1474568 | tf_op jit(solution)/shard_map/ppermute | solution.py:570
  (155 shorter events, 119.5 us)
Async XLA Ops:
  0.0 23.3 %collective-permute-start = (bf16[2,1800,896]{2,1,0:T(8,128)(2,1)}, bf16[2,1800,896]{2,1,0:T(8,128)(2,1)}, u32[]{:S(2)}, u32[]{:S(2)}) collective-permute-start(bf16[2,1800,896]{2,1,0:T(8,128)(2,1)} %bitcast.7), channel_id=1, source_target_pairs={{0,1},{1,0},{2,3},{3,2},{4,5},{5,4},{6,7},{7,6},{8,9},{9,8},{10,11... | collective-permute-start | bytes 19353608 | tf_op jit(solution)/shard_map/ppermute | solution.py:473
  5.0 23.9 %all-to-all-start = ((bf16[8,2,75,300]{3,1,2,0:T(2,128)(2,1)}), bf16[8,2,75,300]{3,1,2,0:T(2,128)(2,1)}, u32[]{:S(2)}, u32[]{:S(2)}) async-start(bf16[8,2,75,300]{3,1,2,0:T(2,128)(2,1)} %broadcast_in_dim.2), calls=%async_computation | async-start | bytes 1843200 | tf_op jit(solution)/shard_map/all_to_all | solution.py:443
  28.8 6.2 %collective-permute-start.2 = (bf16[256,128]{1,0:T(8,128)(2,1)}, bf16[256,128]{1,0:T(8,128)(2,1)S(1)}, u32[]{:S(2)}, u32[]{:S(2)}) collective-permute-start(bf16[256,128]{1,0:T(8,128)(2,1)} %copy-done.34), channel_id=1, source_target_pairs={{0,16},{8,24},{16,0},{24,8},{1,17},{9,25},{17,1},{25,9},{2,18},{10... | collective-permute-start | bytes 196616 | tf_op jit(solution)/shard_map/ppermute | solution.py:449
  36.8 24.9 %all-to-all-start.1 = ((bf16[8,272,128]{2,1,0:T(8,128)(2,1)}), bf16[8,272,128]{2,1,0:T(8,128)(2,1)}, u32[]{:S(2)}, u32[]{:S(2)}) async-start(bf16[8,272,128]{2,1,0:T(8,128)(2,1)} %copy-done.20), calls=%async_computation.1 | async-start | bytes 1114112 | tf_op jit(solution)/shard_map/all_to_all | solution.py:443
  63.3 13.9 %all-to-all-start.2 = ((bf16[8,32,128]{2,1,0:T(8,128)(2,1)}), bf16[8,32,128]{2,1,0:T(8,128)(2,1)S(1)}, u32[]{:S(2)}, u32[]{:S(2)}) async-start(bf16[8,32,128]{2,1,0:T(8,128)(2,1)} %summed.3), calls=%async_computation.2 | async-start | bytes 131072 | tf_op jit(solution)/shard_map/all_to_all | solution.py:443
  80.8 8.2 %collective-permute-start.5 = (bf16[496,128]{1,0:T(8,128)(2,1)S(1)}, bf16[496,128]{1,0:T(8,128)(2,1)S(1)}, u32[]{:S(2)}, u32[]{:S(2)}) collective-permute-start(bf16[496,128]{1,0:T(8,128)(2,1)S(1)} %get-tuple-element.56), channel_id=1, source_target_pairs={{0,16},{8,24},{16,0},{24,8},{1,17},{9,25},{17,1},{25,9},{2,18},{10... | collective-permute-start | bytes 380936 | tf_op jit(solution)/shard_map/ppermute | solution.py:449
  83.3 8.3 %collective-permute-start.6 = (bf16[496,128]{1,0:T(8,128)(2,1)S(1)}, bf16[496,128]{1,0:T(8,128)(2,1)S(1)}, u32[]{:S(2)}, u32[]{:S(2)}) collective-permute-start(bf16[496,128]{1,0:T(8,128)(2,1)S(1)} %get-tuple-element.57), channel_id=1, source_target_pairs={{0,24},{8,16},{16,8},{24,0},{1,25},{9,17},{17,9},{25,1},{2,26},{10... | collective-permute-start | bytes 380936 | tf_op jit(solution)/shard_map/ppermute | solution.py:449
  101.4 6.5 %collective-permute-start.7 = (bf16[960,128]{1,0:T(8,128)(2,1)S(1)}, bf16[960,128]{1,0:T(8,128)(2,1)S(1)}, u32[]{:S(2)}, u32[]{:S(2)}) collective-permute-start(bf16[960,128]{1,0:T(8,128)(2,1)S(1)} %tail.3.refs_0_), channel_id=1, source_target_pairs={{0,2},{2,0},{4,6},{6,4},{1,3},{3,1},{5,7},{7,5},{8,10},{10,8},{12,... | collective-permute-start | bytes 737288 | tf_op jit(solution)/shard_map/ppermute | solution.py:449
  102.3 12.6 %collective-permute-start.8 = (bf16[960,128]{1,0:T(8,128)(2,1)S(1)}, bf16[960,128]{1,0:T(8,128)(2,1)S(1)}, u32[]{:S(2)}, u32[]{:S(2)}) collective-permute-start(bf16[960,128]{1,0:T(8,128)(2,1)S(1)} %tail.3.refs_0_), channel_id=1, source_target_pairs={{0,4},{2,6},{4,0},{6,2},{1,5},{3,7},{5,1},{7,3},{8,12},{10,14},{12... | collective-permute-start | bytes 737288 | tf_op jit(solution)/shard_map/ppermute | solution.py:449
  104.7 12.8 %collective-permute-start.9 = (bf16[960,128]{1,0:T(8,128)(2,1)S(1)}, bf16[960,128]{1,0:T(8,128)(2,1)S(1)}, u32[]{:S(2)}, u32[]{:S(2)}) collective-permute-start(bf16[960,128]{1,0:T(8,128)(2,1)S(1)} %tail.3.refs_0_), channel_id=1, source_target_pairs={{0,6},{2,4},{4,2},{6,0},{1,7},{3,5},{5,3},{7,1},{8,14},{10,12},{12... | collective-permute-start | bytes 737288 | tf_op jit(solution)/shard_map/ppermute | solution.py:449
  123.6 5.4 %collective-permute-start.11 = (bf16[256,128]{1,0:T(8,128)(2,1)S(1)}, bf16[256,128]{1,0:T(8,128)(2,1)S(1)}, u32[]{:S(2)}, u32[]{:S(2)}) collective-permute-start(bf16[256,128]{1,0:T(8,128)(2,1)S(1)} %get-tuple-element.61), channel_id=1, source_target_pairs={{0,16},{8,24},{16,0},{24,8},{1,17},{9,25},{17,1},{25,9},{2,18},{10... | collective-permute-start | bytes 196616 | tf_op jit(solution)/shard_map/ppermute | solution.py:449
  124.0 5.4 %collective-permute-start.12 = (bf16[256,128]{1,0:T(8,128)(2,1)S(1)}, bf16[256,128]{1,0:T(8,128)(2,1)S(1)}, u32[]{:S(2)}, u32[]{:S(2)}) collective-permute-start(bf16[256,128]{1,0:T(8,128)(2,1)S(1)} %get-tuple-element.62), channel_id=1, source_target_pairs={{0,24},{8,16},{16,8},{24,0},{1,25},{9,17},{17,9},{25,1},{2,26},{10... | collective-permute-start | bytes 196616 | tf_op jit(solution)/shard_map/ppermute | solution.py:449
  150.6 11.6 %all-to-all-start.4 = ((bf16[8,32,128]{2,1,0:T(8,128)(2,1)}), bf16[8,32,128]{2,1,0:T(8,128)(2,1)S(1)}, u32[]{:S(2)}, u32[]{:S(2)}) async-start(bf16[8,32,128]{2,1,0:T(8,128)(2,1)} %summed.4), calls=%async_computation.4 | async-start | bytes 131072 | tf_op jit(solution)/shard_map/all_to_all | solution.py:443
  163.3 7.9 %collective-permute-start.14 = (bf16[496,128]{1,0:T(8,128)(2,1)S(1)}, bf16[496,128]{1,0:T(8,128)(2,1)S(1)}, u32[]{:S(2)}, u32[]{:S(2)}) collective-permute-start(bf16[496,128]{1,0:T(8,128)(2,1)S(1)} %get-tuple-element.66), channel_id=1, source_target_pairs={{0,16},{8,24},{16,0},{24,8},{1,17},{9,25},{17,1},{25,9},{2,18},{10... | collective-permute-start | bytes 380936 | tf_op jit(solution)/shard_map/ppermute | solution.py:449
  182.4 5.1 %collective-permute-start.16 = (bf16[960,128]{1,0:T(8,128)(2,1)S(1)}, bf16[960,128]{1,0:T(8,128)(2,1)S(1)}, u32[]{:S(2)}, u32[]{:S(2)}) collective-permute-start(bf16[960,128]{1,0:T(8,128)(2,1)S(1)} %tail.4.refs_0_), channel_id=1, source_target_pairs={{0,2},{2,0},{4,6},{6,4},{1,3},{3,1},{5,7},{7,5},{8,10},{10,8},{12,... | collective-permute-start | bytes 737288 | tf_op jit(solution)/shard_map/ppermute | solution.py:449
  182.5 8.1 %collective-permute-start.17 = (bf16[960,128]{1,0:T(8,128)(2,1)S(1)}, bf16[960,128]{1,0:T(8,128)(2,1)S(1)}, u32[]{:S(2)}, u32[]{:S(2)}) collective-permute-start(bf16[960,128]{1,0:T(8,128)(2,1)S(1)} %tail.4.refs_0_), channel_id=1, source_target_pairs={{0,4},{2,6},{4,0},{6,2},{1,5},{3,7},{5,1},{7,3},{8,12},{10,14},{12... | collective-permute-start | bytes 737288 | tf_op jit(solution)/shard_map/ppermute | solution.py:449
  184.3 8.8 %collective-permute-start.18 = (bf16[960,128]{1,0:T(8,128)(2,1)S(1)}, bf16[960,128]{1,0:T(8,128)(2,1)S(1)}, u32[]{:S(2)}, u32[]{:S(2)}) collective-permute-start(bf16[960,128]{1,0:T(8,128)(2,1)S(1)} %tail.4.refs_0_), channel_id=1, source_target_pairs={{0,6},{2,4},{4,2},{6,0},{1,7},{3,5},{5,3},{7,1},{8,14},{10,12},{12... | collective-permute-start | bytes 737288 | tf_op jit(solution)/shard_map/ppermute | solution.py:449
  223.4 10.5 %all-to-all-start.6 = ((bf16[8,32,128]{2,1,0:T(8,128)(2,1)}), bf16[8,32,128]{2,1,0:T(8,128)(2,1)S(1)}, u32[]{:S(2)}, u32[]{:S(2)}) async-start(bf16[8,32,128]{2,1,0:T(8,128)(2,1)} %summed.5), calls=%async_computation.6 | async-start | bytes 131072 | tf_op jit(solution)/shard_map/all_to_all | solution.py:443
  235.0 6.9 %collective-permute-start.23 = (bf16[496,128]{1,0:T(8,128)(2,1)S(1)}, bf16[496,128]{1,0:T(8,128)(2,1)S(1)}, u32[]{:S(2)}, u32[]{:S(2)}) collective-permute-start(bf16[496,128]{1,0:T(8,128)(2,1)S(1)} %get-tuple-element.76), channel_id=1, source_target_pairs={{0,16},{8,24},{16,0},{24,8},{1,17},{9,25},{17,1},{25,9},{2,18},{10... | collective-permute-start | bytes 380936 | tf_op jit(solution)/shard_map/ppermute | solution.py:449
  238.3 5.3 %collective-permute-start.24 = (bf16[496,128]{1,0:T(8,128)(2,1)S(1)}, bf16[496,128]{1,0:T(8,128)(2,1)S(1)}, u32[]{:S(2)}, u32[]{:S(2)}) collective-permute-start(bf16[496,128]{1,0:T(8,128)(2,1)S(1)} %get-tuple-element.77), channel_id=1, source_target_pairs={{0,24},{8,16},{16,8},{24,0},{1,25},{9,17},{17,9},{25,1},{2,26},{10... | collective-permute-start | bytes 380936 | tf_op jit(solution)/shard_map/ppermute | solution.py:449
  253.4 5.1 %collective-permute-start.25 = (bf16[960,128]{1,0:T(8,128)(2,1)S(1)}, bf16[960,128]{1,0:T(8,128)(2,1)S(1)}, u32[]{:S(2)}, u32[]{:S(2)}) collective-permute-start(bf16[960,128]{1,0:T(8,128)(2,1)S(1)} %tail.5.refs_0_), channel_id=1, source_target_pairs={{0,2},{2,0},{4,6},{6,4},{1,3},{3,1},{5,7},{7,5},{8,10},{10,8},{12,... | collective-permute-start | bytes 737288 | tf_op jit(solution)/shard_map/ppermute | solution.py:449
  253.5 9.5 %collective-permute-start.26 = (bf16[960,128]{1,0:T(8,128)(2,1)S(1)}, bf16[960,128]{1,0:T(8,128)(2,1)S(1)}, u32[]{:S(2)}, u32[]{:S(2)}) collective-permute-start(bf16[960,128]{1,0:T(8,128)(2,1)S(1)} %tail.5.refs_0_), channel_id=1, source_target_pairs={{0,4},{2,6},{4,0},{6,2},{1,5},{3,7},{5,1},{7,3},{8,12},{10,14},{12... | collective-permute-start | bytes 737288 | tf_op jit(solution)/shard_map/ppermute | solution.py:449
  256.8 8.8 %collective-permute-start.27 = (bf16[960,128]{1,0:T(8,128)(2,1)S(1)}, bf16[960,128]{1,0:T(8,128)(2,1)S(1)}, u32[]{:S(2)}, u32[]{:S(2)}) collective-permute-start(bf16[960,128]{1,0:T(8,128)(2,1)S(1)} %tail.5.refs_0_), channel_id=1, source_target_pairs={{0,6},{2,4},{4,2},{6,0},{1,7},{3,5},{5,3},{7,1},{8,14},{10,12},{12... | collective-permute-start | bytes 737288 | tf_op jit(solution)/shard_map/ppermute | solution.py:449
  267.1 16.0 %collective-permute-start.28 = (f32[960,128]{1,0:T(8,128)S(1)}, f32[960,128]{1,0:T(8,128)S(1)}, u32[]{:S(2)}, u32[]{:S(2)}) collective-permute-start(f32[960,128]{1,0:T(8,128)S(1)} %last.1.mine_ref), channel_id=1, source_target_pairs={{0,1},{1,0},{2,3},{3,2},{4,5},{5,4},{6,7},{7,6},{8,9},{9,8},{10,11... | collective-permute-start | bytes 1474568 | tf_op jit(solution)/shard_map/ppermute | solution.py:570
  (48 other events, 324.2 us)
where the time goes:
time: 287 us; the launch traced here: 286 us
  starting transfers between devices  79.9 us (28%)
  waiting for transfers between devices  71.4 us (25%)
  Pallas kernels  54.7 us (19%)
  local copies, waits for them, and re-layouts  43.1 us (15%)
  blocking collectives  36.3 us (13%)
    ppermute x27, waiting for transfers between devices, swapped(): lax.ppermute(values[k], axis, [(i, i ^ k) for i in range(size)])  52.1 us
    ppermute x27, starting transfers between devices, swapped(): lax.ppermute(values[k], axis, [(i, i ^ k) for i in range(size)])  37 us
    all_to_all x2, blocking collectives, exchange(): return lax.all_to_all(copies, axis, 0, 0, tiled=True)  36.3 us
    unnamed x77, local copies, waits for them, and re-layouts  30.6 us
    all_to_all x5, starting transfers between devices, exchange(): return lax.all_to_all(copies, axis, 0, 0, tiled=True)  25.1 us
    pallas_call x3, Pallas kernels, per_device(): recv = swapped([tail(*mixed, own, other)] * nx, 'x')  21 us
    all_to_all x5, waiting for transfers between devices, exchange(): return lax.all_to_all(copies, axis, 0, 0, tiled=True)  17.9 us
    ppermute x1, starting transfers between devices, per_device(): return output(state, lax.ppermute(state, 'c', swap))  14.5 us
  transfers between devices with their start and end apart: 34, of which 25 were waited for; matrix products, arithmetic and copies ran while one was open for 5% of the time, Pallas kernels for 6%

commit v1 on v0

--- a/solution.py
+++ b/solution.py
@@ -18,6 +18,7 @@
 CHUNK = 256
 STRIPS = 4
 LARGE = 36 << 20
+MIDDLE = 20 << 20
 SMALL = 12 << 20
 
 
@@ -53,11 +54,6 @@
 
 def buffer_rows(rows):
     return rows + steps_of(rows) * CHUNK
-
-
-def strips(rows, width):
-    depth = 2 * rows // STRIPS
-    return [[(at, min(at + depth, width))] for at in range(0, width, depth)]
 
 
 def pairs_of(rows, width):
@@ -133,7 +129,7 @@
         share_ref[i * low : (i + 2) * low, :] = jnp.concatenate(both, axis=0).astype(BF16)
 
 
-def overlap(state_ref, pieces_ref, buf, acc, across, copies):
+def overlap(state_ref, pieces_ref, buf, acc, across, copies=()):
     rows = state_ref.shape[0]
     value = state_ref[...].T
     spare = jnp.zeros((64, across.shape[3] - rows), F32)
@@ -146,7 +142,7 @@
     count = buf.shape[0]
     acc[...] = jnp.zeros(acc.shape, F32)
 
-    @pl.loop(0, len(copies))
+    @pl.loop(0, steps_of(rows))
     def _(n):
         wait_for(copies, n)
         here = pl.ds(pl.multiple_of(n * CHUNK, CHUNK), CHUNK)
@@ -222,6 +218,20 @@
             start_ref[pl.ds(t, low, stride=act), :] = value * inverse
 
 
+def stage_kernel(after, own, other, buf, zeros, sems):
+    width = own.shape[1]
+    zeros[...] = jnp.zeros(zeros.shape, BF16)
+    copies = []
+    for s, ref in enumerate((own, other)):
+        copies.append(pltpu.make_async_copy(ref, buf.at[s, :, pl.ds(0, width), :], sems.at[s, 0]))
+        there = buf.at[s, :, pl.ds(width, zeros.shape[1]), :]
+        copies.append(pltpu.make_async_copy(zeros, there, sems.at[s, 1]))
+    for copy in copies:
+        copy.start()
+    for copy in copies:
+        copy.wait()
+
+
 def opening_kernel(
     act, source_ref, vir_ref, act_ref, pair_ref, own,
     start_ref, inv_ref, share_ref, pieces_ref, *scratch,
@@ -243,12 +253,11 @@
 
 
 def next_kernel(act, nx, *refs):
-    prev_ref, kron_ref, start_ref, inv_ref, own, other, state_ref, share_ref, *rest = refs[nx:]
-    *outs, pieces, buf, sems, acc, across = rest
-    copies = fetches([own, other], buf, sems, pairs_of(start_ref.shape[0], own.shape[1]))
+    prev_ref, kron_ref, start_ref, inv_ref, buf, state_ref, share_ref, *rest = refs[nx:]
+    *outs, pieces, acc, across = rest
     set_updated(state_ref, refs[:nx], prev_ref, kron_ref, start_ref, inv_ref, act)
     set_share(state_ref, share_ref, act)
-    overlap(state_ref, pieces, buf, acc, across, copies)
+    overlap(state_ref, pieces, buf, acc, across)
     spread(pieces, outs)
 
 
@@ -364,9 +373,9 @@
 
 
 def tail_kernel(act, height, *refs):
-    *recvs, own, other, out_ref, inter_ref, both, total, right, recv_sems, buf, sems = refs
+    *recvs, buf, out_ref, inter_ref, both, total, right, recv_sems = refs
     rows = out_ref.shape[0]
-    nfit = own.shape[2]
+    nfit = buf.shape[3]
     me = lax.axis_index("y")
     moves = [
         pltpu.make_async_copy(recv, inter_ref.at[me ^ k], recv_sems.at[k])
@@ -374,7 +383,6 @@
     ]
     for move in moves:
         move.start()
-    copies = fetches([own, other], buf, sems, strips(rows, own.shape[1]))
     for move in moves:
         move.wait()
     wide = inter_ref.shape[0] * height // LANES
@@ -396,9 +404,8 @@
 
     depth = 2 * rows // STRIPS
 
-    @pl.loop(0, len(copies))
+    @pl.loop(0, STRIPS)
     def _(n):
-        wait_for(copies, n)
         there = pl.ds(pl.multiple_of(n * depth, 16), depth)
         here = None
         for s in range(2):
@@ -422,18 +429,19 @@
 
 
 VMEM = pl.BlockSpec(memory_space=pltpu.VMEM)
+ANY = pl.BlockSpec(memory_space=pl.ANY)
 HBM = pl.BlockSpec(memory_space=pltpu.HBM)
 SMEM = pl.BlockSpec(memory_space=pltpu.SMEM)
 
 
-def call(body, outs, ins, scratch=(), name=None, flops=0, moved=0):
+def call(body, outs, ins, scratch=(), name=None, flops=0, moved=0, limit=LARGE, out=VMEM):
     return pl.pallas_call(
         body,
         out_shape=outs,
         in_specs=ins,
-        out_specs=jax.tree.map(lambda _: VMEM, outs),
+        out_specs=jax.tree.map(lambda _: out, outs),
         scratch_shapes=scratch,
-        compiler_params=pltpu.CompilerParams(vmem_limit_bytes=LARGE if flops else SMALL),
+        compiler_params=pltpu.CompilerParams(vmem_limit_bytes=limit if moved else SMALL),
         cost_estimate=pl.CostEstimate(flops=flops, bytes_accessed=moved, transcendentals=0),
         name=name,
     )
@@ -516,7 +524,16 @@
     )
     later = call(
         functools.partial(next_kernel, act, nx), [state_shape, share_shape] + piece_shape,
-        [VMEM] * (nx + 4) + [HBM] * 2, [pieces] + sums(2), "later", flops, moved,
+        [VMEM] * (nx + 5), [pieces] + sums(2)[2:], "later", flops, moved // 4, MIDDLE,
+    )
+    stage = call(
+        stage_kernel, jax.ShapeDtypeStruct((2, 2, buffer_rows(rows), nfit), BF16),
+        [ANY, HBM, HBM],
+        [
+            pltpu.VMEM((2, buffer_rows(rows) - width, nfit), BF16),
+            pltpu.SemaphoreType.DMA((2, 2)),
+        ],
+        "stage", 0, 4 * moved, 4 << 20, ANY,
     )
     last = call(
         functools.partial(last_kernel, act, nx), state_shape, [VMEM] * (nx + 4), (), "last"
@@ -535,16 +552,15 @@
     )
     tail = call(
         functools.partial(tail_kernel, act, height), sent(rows),
-        [HBM] * (ny + 2),
+        [HBM] * ny + [VMEM],
         [
             pltpu.VMEM((ny, height + extra, LANES), BF16),
             pltpu.VMEM((2 * rows, LANES), F32),
             pltpu.VMEM((rows, LANES), F32),
             pltpu.VMEM((2, 2, LANES, nfit), BF16),
             pltpu.SemaphoreType.DMA((ny,)),
-        ]
-        + fetch(2),
-        "tail", flops, moved,
+        ],
+        "tail", flops, moved // 4, MIDDLE,
     )
     output = call(
         functools.partial(output_kernel, act),
@@ -561,11 +577,12 @@
             part, couple = lax.optimization_barrier((part, couple))
             couple = laid_out(couple, low, ny)
         else:
-            state, share_now, *part = later(*recv, state, kron, start, inverse, own, other)
+            state, share_now, *part = later(*recv, state, kron, start, inverse, blocks)
         mixed = exchange(along_z(*swapped(part, "y"), share_now), "z")
         inter = exchange(summed(mixed), "z")
-        mixed = swapped(along_y(inter, coupled(mixed, couple)), "y")
-        recv = swapped([tail(*mixed, own, other)] * nx, "x")
+        mixed = along_y(inter, coupled(mixed, couple))
+        blocks = stage(mixed[0], own, other)
+        recv = swapped([tail(*swapped(mixed, "y"), blocks)] * nx, "x")
     state = last(*recv, state, kron, start, inverse)
     return output(state, lax.ppermute(state, "c", swap))
 

time: 287 us -> 249 us (0.87)
  local copies, waits for them, and re-layouts: 43.1 us -> 23.4 us
  waiting for transfers between devices: 71.4 us -> 54.1 us
    ppermute x27, waiting for transfers between devices: 52.1 us -> 26.7 us  [swapped(): lax.ppermute(values[k], axis, [(i, i ^ k) for i in range(size)])]
    unnamed x77 -> x39, local copies, waits for them, and re-layouts: 30.6 us -> 11.6 us
    all_to_all x5, waiting for transfers between devices: 17.9 us -> 26 us  [exchange(): return lax.all_to_all(copies, axis, 0, 0, tiled=True)]
    pallas_call x11 -> x14, Pallas kernels: 39.8 us -> 41.2 us  [the longest x3 15.6 us: per_device(): recv = swapped([tail(*swapped(mixed, 'y'), blocks)] * nx, 'x')]
  transfers between devices with their start and end apart: 34 -> 34, of which waited for: 25 -> 18; matrix products, arithmetic and copies ran while one was open for 5% -> 4% of each run, Pallas kernels for 6% -> 10%
where the time goes in v1:
time: 249 us; the launch traced here: 248 us
  starting transfers between devices  79.9 us (32%)
  Pallas kernels  55.9 us (22%)
  waiting for transfers between devices  54.1 us (22%)
  blocking collectives  34.4 us (14%)
  local copies, waits for them, and re-layouts  23.4 us (9%)
    ppermute x27, starting transfers between devices, swapped(): lax.ppermute(values[k], axis, [(i, i ^ k) for i in range(size)])  37.1 us
    all_to_all x2, blocking collectives, exchange(): return lax.all_to_all(copies, axis, 0, 0, tiled=True)  34.4 us
    ppermute x27, waiting for transfers between devices, swapped(): lax.ppermute(values[k], axis, [(i, i ^ k) for i in range(size)])  26.7 us
    all_to_all x5, waiting for transfers between devices, exchange(): return lax.all_to_all(copies, axis, 0, 0, tiled=True)  26 us
    all_to_all x5, starting transfers between devices, exchange(): return lax.all_to_all(copies, axis, 0, 0, tiled=True)  24.1 us
    pallas_call x3, Pallas kernels, per_device(): recv = swapped([tail(*swapped(mixed, 'y'), blocks)] * nx, 'x')  15.6 us
    ppermute x1, starting transfers between devices, per_device(): return output(state, lax.ppermute(state, 'c', swap))  15.4 us
    unnamed x39, local copies, waits for them, and re-layouts  11.6 us
  transfers between devices with their start and end apart: 34, of which 18 were waited for; matrix products, arithmetic and copies ran while one was open for 4% of the time, Pallas kernels for 10%

profile of v1, /device:TPU:1, one launch (start us, length us, event | category | flops | bytes accessed | tf_op | source)
XLA Modules:
  0.0 248.1 jit_solution(9167191428026242658)
XLA Ops:
  5.0 5.8 %all-to-all-start = ((bf16[8,2,75,300]{3,1,2,0:T(2,128)(2,1)}), bf16[8,2,75,300]{3,1,2,0:T(2,128)(2,1)}, u32[]{:S(2)}, u32[]{:S(2)}) async-start(bf16[8,2,75,300]{3,1,2,0:T(2,128)(2,1)} %broadcast_in_dim.2), calls=%async_computation | async-start | bytes 1843200 | tf_op jit(solution)/shard_map/all_to_all | solution.py:451
  14.1 5.0 %opening.1 = (f32[960,128]{1,0:T(8,128)S(1)}, f32[960,128]{1,0:T(8,128)S(1)}, bf16[240,128]{1,0:T(8,128)(2,1)S(1)}, bf16[2,256,128]{2,1,0:T(8,128)(2,1)S(1)}) custom-call(f32[2,75,1536]{2,1,0:T(8,128)S(1)} %copy.12.source_ref, f32[75,1]{1,0:T(8,128)S(1)} %copy.13.vir_ref, f32[24]{0:T(128)S(1)} %copy-done.15, f32[1,128]{1,0:T(1,128)S(1)} %reshape_tile.3.pair_ref, ...), custom_call_target="tpu_custom_call" | custom-call | flops 412876800 | bytes 6451200 | tf_op jit(solution)/shard_map/opening/pallas_call | solution.py:572
  19.1 3.7 %second.1 = (bf16[256,128]{1,0:T(8,128)(2,1)S(1)}, bf16[256,128]{1,0:T(8,128)(2,1)S(1)}, bf16[256,128]{1,0:T(8,128)(2,1)S(1)}, bf16[256,128]{1,0:T(8,128)(2,1)S(1)}) custom-call(f32[960,128]{1,0:T(8,128)S(1)} %get-tuple-element.42.start_ref.refs_4_.refs_6_, bf16[2,256,128]{2,1,0:T(8,128)(2,1)S(1)} %get-tuple-element.43.first_ref, ...), custom_call_target="tpu_custom_call" | custom-call | flops 412876800 | bytes 6451200 | tf_op jit(solution)/shard_map/second/pallas_call | solution.py:576
  32.4 8.2 %all-to-all-start.1 = ((bf16[8,272,128]{2,1,0:T(8,128)(2,1)}), bf16[8,272,128]{2,1,0:T(8,128)(2,1)S(1)}, u32[]{:S(2)}, u32[]{:S(2)}) async-start(bf16[8,272,128]{2,1,0:T(8,128)(2,1)} %along_z.3), calls=%async_computation.1 | async-start | bytes 1114112 | tf_op jit(solution)/shard_map/all_to_all | solution.py:451
  40.6 3.4 %copy.16 = bf16[8,2,75,300]{2,0,3,1:T(8,128)(2,1)} copy(bf16[8,2,75,300]{3,1,2,0:T(2,128)(2,1)} %all-to-all-done) | data formatting | bytes 1440000 | tf_op jit(solution)/shard_map/reshape | solution.py:463
  44.0 12.1 %all-to-all-done.1.recv_ref = bf16[8,272,128]{2,1,0:T(8,128)(2,1)S(1)} async-done(((bf16[8,272,128]{2,1,0:T(8,128)(2,1)}), bf16[8,272,128]{2,1,0:T(8,128)(2,1)S(1)}, u32[]{:S(2)}, u32[]{:S(2)}) %all-to-all-start.1) | async-done | bytes 557088 | tf_op jit(solution)/shard_map/all_to_all | solution.py:451
  74.1 3.6 %stage.3.refs_4_.refs_8_ = bf16[2,2,1984,896]{3,2,1,0:T(8,128)(2,1)S(1)} custom-call(bf16[496,128]{1,0:T(8,128)(2,1)S(1)} %get-tuple-element.54.after.refs_0_, bf16[2,1800,896]{2,1,0:T(8,128)(2,1)S(1)} %bitcast.9, bf16[2,1800,896]{2,1,0:T(8,128)(2,1)} %collective-permute-done.other), custom_call_target="tpu_custom_call" | custom-call | bytes 51609600 | tf_op jit(solution)/shard_map/stage/pallas_call | solution.py:584
  77.7 5.2 %tail.3.refs_0_ = bf16[960,128]{1,0:T(8,128)(2,1)S(1)} custom-call(bf16[496,128]{1,0:T(8,128)(2,1)S(1)} %get-tuple-element.54.after.refs_0_, bf16[496,128]{1,0:T(8,128)(2,1)S(1)} %collective-permute-done.4.refs_1_, bf16[496,128]{1,0:T(8,128)(2,1)S(1)} %collective-permute-done.5.refs_2_, bf16[496,128]{1,0:T(8,128)(2,1)S(1)} %collective-permute-done.6.refs_3_, ...), custom_call_target="tpu_custom_call" | custom-call | flops 825753600 | bytes 3225600 | tf_op jit(solution)/shard_map/tail/pallas_call | solution.py:585
  87.0 4.8 %collective-permute-done.9.refs_3_ = bf16[960,128]{1,0:T(8,128)(2,1)S(1)} collective-permute-done((bf16[960,128]{1,0:T(8,128)(2,1)S(1)}, bf16[960,128]{1,0:T(8,128)(2,1)S(1)}, u32[]{:S(2)}, u32[]{:S(2)}) %collective-permute-start.9) | collective-permute-done | bytes 245792 | tf_op jit(solution)/shard_map/ppermute | solution.py:457
  92.6 4.4 %later.2 = (f32[960,128]{1,0:T(8,128)S(1)}, bf16[240,128]{1,0:T(8,128)(2,1)S(1)}, bf16[256,128]{1,0:T(8,128)(2,1)S(1)}, bf16[256,128]{1,0:T(8,128)(2,1)S(1)}, bf...) custom-call(bf16[960,128]{1,0:T(8,128)(2,1)S(1)} %tail.3.refs_0_, ...), custom_call_target="tpu_custom_call" | custom-call | flops 825753600 | bytes 3225600 | tf_op jit(solution)/shard_map/later/pallas_call | solution.py:580
  97.7 4.8 %collective-permute-start.11 = (bf16[256,128]{1,0:T(8,128)(2,1)S(1)}, bf16[256,128]{1,0:T(8,128)(2,1)S(1)}, u32[]{:S(2)}, u32[]{:S(2)}) collective-permute-start(bf16[256,128]{1,0:T(8,128)(2,1)S(1)} %get-tuple-element.61), channel_id=1, source_target_pairs={{0,16},{8,24},{16,0},{24,8},{1,17},{9,25},{17,1},{25,9},{2,18},{10... | collective-permute-start | bytes 196616 | tf_op jit(solution)/shard_map/ppermute | solution.py:457
  106.9 19.5 %all_to_all.35.recv_ref = bf16[8,272,128]{2,1,0:T(8,128)(2,1)S(1)} all-to-all(bf16[8,272,128]{2,1,0:T(8,128)(2,1)S(1)} %along_z.4), channel_id=1, replica_groups=mesh['z'=8,'y'=4,'x'=4,'c'=2] {'z'}, dimensions={0} | all-to-all | bytes 1114112 | tf_op jit(solution)/shard_map/all_to_all | solution.py:451
  127.0 3.4 %all-to-all-start.4 = ((bf16[8,32,128]{2,1,0:T(8,128)(2,1)}), bf16[8,32,128]{2,1,0:T(8,128)(2,1)S(1)}, u32[]{:S(2)}, u32[]{:S(2)}) async-start(bf16[8,32,128]{2,1,0:T(8,128)(2,1)} %summed.4), calls=%async_computation.4 | async-start | bytes 131072 | tf_op jit(solution)/shard_map/all_to_all | solution.py:451
  132.4 5.2 %all-to-all-done.4.inter_ref = bf16[8,32,128]{2,1,0:T(8,128)(2,1)S(1)} async-done(((bf16[8,32,128]{2,1,0:T(8,128)(2,1)}), bf16[8,32,128]{2,1,0:T(8,128)(2,1)S(1)}, u32[]{:S(2)}, u32[]{:S(2)}) %all-to-all-start.4) | async-done | bytes 65568 | tf_op jit(solution)/shard_map/all_to_all | solution.py:451
  144.5 3.6 %stage.4.refs_4_.refs_8_ = bf16[2,2,1984,896]{3,2,1,0:T(8,128)(2,1)S(1)} custom-call(bf16[496,128]{1,0:T(8,128)(2,1)S(1)} %get-tuple-element.64.after.refs_0_, bf16[2,1800,896]{2,1,0:T(8,128)(2,1)S(1)} %bitcast.10, bf16[2,1800,896]{2,1,0:T(8,128)(2,1)} %collective-permute-done.other), custom_call_target="tpu_custom_call" | custom-call | bytes 51609600 | tf_op jit(solution)/shard_map/stage/pallas_call | solution.py:584
  148.1 5.2 %tail.4.refs_0_ = bf16[960,128]{1,0:T(8,128)(2,1)S(1)} custom-call(bf16[496,128]{1,0:T(8,128)(2,1)S(1)} %get-tuple-element.64.after.refs_0_, bf16[496,128]{1,0:T(8,128)(2,1)S(1)} %collective-permute-done.13.refs_1_, bf16[496,128]{1,0:T(8,128)(2,1)S(1)} %collective-permute-done.14.refs_2_, bf16[496,128]{1,0:T(8,128)(2,1)S(1)} %collective-permute-done.15.refs_3_, ...), custom_call_target="tpu_custom_call" | custom-call | flops 825753600 | bytes 3225600 | tf_op jit(solution)/shard_map/tail/pallas_call | solution.py:585
  158.1 4.2 %collective-permute-done.18.refs_3_ = bf16[960,128]{1,0:T(8,128)(2,1)S(1)} collective-permute-done((bf16[960,128]{1,0:T(8,128)(2,1)S(1)}, bf16[960,128]{1,0:T(8,128)(2,1)S(1)}, u32[]{:S(2)}, u32[]{:S(2)}) %collective-permute-start.18) | collective-permute-done | bytes 245792 | tf_op jit(solution)/shard_map/ppermute | solution.py:457
  163.9 4.5 %later.3 = (f32[960,128]{1,0:T(8,128)S(1)}, bf16[240,128]{1,0:T(8,128)(2,1)S(1)}, bf16[256,128]{1,0:T(8,128)(2,1)S(1)}, bf16[256,128]{1,0:T(8,128)(2,1)S(1)}, bf...) custom-call(bf16[960,128]{1,0:T(8,128)(2,1)S(1)} %tail.4.refs_0_, ...), custom_call_target="tpu_custom_call" | custom-call | flops 825753600 | bytes 3225600 | tf_op jit(solution)/shard_map/later/pallas_call | solution.py:580
  174.6 14.9 %all_to_all.36.recv_ref = bf16[8,272,128]{2,1,0:T(8,128)(2,1)S(1)} all-to-all(bf16[8,272,128]{2,1,0:T(8,128)(2,1)S(1)} %along_z.5), channel_id=1, replica_groups=mesh['z'=8,'y'=4,'x'=4,'c'=2] {'z'}, dimensions={0} | all-to-all | bytes 1114112 | tf_op jit(solution)/shard_map/all_to_all | solution.py:451
  195.4 6.5 %all-to-all-done.6.inter_ref = bf16[8,32,128]{2,1,0:T(8,128)(2,1)S(1)} async-done(((bf16[8,32,128]{2,1,0:T(8,128)(2,1)}), bf16[8,32,128]{2,1,0:T(8,128)(2,1)S(1)}, u32[]{:S(2)}, u32[]{:S(2)}) %all-to-all-start.6) | async-done | bytes 65568 | tf_op jit(solution)/shard_map/all_to_all | solution.py:451
  208.7 3.6 %stage.5.refs_4_ = bf16[2,2,1984,896]{3,2,1,0:T(8,128)(2,1)S(1)} custom-call(bf16[496,128]{1,0:T(8,128)(2,1)S(1)} %get-tuple-element.74.after.refs_0_, bf16[2,1800,896]{2,1,0:T(8,128)(2,1)S(1)} %bitcast.11, bf16[2,1800,896]{2,1,0:T(8,128)(2,1)} %collective-permute-done.other), custom_call_target="tpu_custom_call" | custom-call | bytes 51609600 | tf_op jit(solution)/shard_map/stage/pallas_call | solution.py:584
  212.4 5.2 %tail.5.refs_0_ = bf16[960,128]{1,0:T(8,128)(2,1)S(1)} custom-call(bf16[496,128]{1,0:T(8,128)(2,1)S(1)} %get-tuple-element.74.after.refs_0_, bf16[496,128]{1,0:T(8,128)(2,1)S(1)} %collective-permute-done.22.refs_1_, bf16[496,128]{1,0:T(8,128)(2,1)S(1)} %collective-permute-done.23.refs_2_, bf16[496,128]{1,0:T(8,128)(2,1)S(1)} %collective-permute-done.24.refs_3_, ...), custom_call_target="tpu_custom_call" | custom-call | flops 825753600 | bytes 3225600 | tf_op jit(solution)/shard_map/tail/pallas_call | solution.py:585
  221.3 5.2 %collective-permute-done.27.refs_3_ = bf16[960,128]{1,0:T(8,128)(2,1)S(1)} collective-permute-done((bf16[960,128]{1,0:T(8,128)(2,1)S(1)}, bf16[960,128]{1,0:T(8,128)(2,1)S(1)}, u32[]{:S(2)}, u32[]{:S(2)}) %collective-permute-start.27) | collective-permute-done | bytes 245792 | tf_op jit(solution)/shard_map/ppermute | solution.py:457
  228.6 15.4 %collective-permute-start.28 = (f32[960,128]{1,0:T(8,128)S(1)}, f32[960,128]{1,0:T(8,128)S(1)}, u32[]{:S(2)}, u32[]{:S(2)}) collective-permute-start(f32[960,128]{1,0:T(8,128)S(1)} %last.1.mine_ref), channel_id=1, source_target_pairs={{0,1},{1,0},{2,3},{3,2},{4,5},{5,4},{6,7},{7,6},{8,9},{9,8},{10,11... | collective-permute-start | bytes 1474568 | tf_op jit(solution)/shard_map/ppermute | solution.py:587
  (120 shorter events, 90.5 us)
Async XLA Ops:
  0.0 19.1 %collective-permute-start = (bf16[2,1800,896]{2,1,0:T(8,128)(2,1)}, bf16[2,1800,896]{2,1,0:T(8,128)(2,1)}, u32[]{:S(2)}, u32[]{:S(2)}) collective-permute-start(bf16[2,1800,896]{2,1,0:T(8,128)(2,1)} %bitcast.7), channel_id=1, source_target_pairs={{0,1},{1,0},{2,3},{3,2},{4,5},{5,4},{6,7},{7,6},{8,9},{9,8},{10,11... | collective-permute-start | bytes 19353608 | tf_op jit(solution)/shard_map/ppermute | solution.py:481
  5.0 19.7 %all-to-all-start = ((bf16[8,2,75,300]{3,1,2,0:T(2,128)(2,1)}), bf16[8,2,75,300]{3,1,2,0:T(2,128)(2,1)}, u32[]{:S(2)}, u32[]{:S(2)}) async-start(bf16[8,2,75,300]{3,1,2,0:T(2,128)(2,1)} %broadcast_in_dim.2), calls=%async_computation | async-start | bytes 1843200 | tf_op jit(solution)/shard_map/all_to_all | solution.py:451
  32.4 23.7 %all-to-all-start.1 = ((bf16[8,272,128]{2,1,0:T(8,128)(2,1)}), bf16[8,272,128]{2,1,0:T(8,128)(2,1)S(1)}, u32[]{:S(2)}, u32[]{:S(2)}) async-start(bf16[8,272,128]{2,1,0:T(8,128)(2,1)} %along_z.3), calls=%async_computation.1 | async-start | bytes 1114112 | tf_op jit(solution)/shard_map/all_to_all | solution.py:451
  56.7 10.5 %all-to-all-start.2 = ((bf16[8,32,128]{2,1,0:T(8,128)(2,1)}), bf16[8,32,128]{2,1,0:T(8,128)(2,1)S(1)}, u32[]{:S(2)}, u32[]{:S(2)}) async-start(bf16[8,32,128]{2,1,0:T(8,128)(2,1)} %summed.3), calls=%async_computation.2 | async-start | bytes 131072 | tf_op jit(solution)/shard_map/all_to_all | solution.py:451
  67.3 10.4 %collective-permute-start.4 = (bf16[496,128]{1,0:T(8,128)(2,1)S(1)}, bf16[496,128]{1,0:T(8,128)(2,1)S(1)}, u32[]{:S(2)}, u32[]{:S(2)}) collective-permute-start(bf16[496,128]{1,0:T(8,128)(2,1)S(1)} %get-tuple-element.55), channel_id=1, source_target_pairs={{0,8},{8,0},{16,24},{24,16},{1,9},{9,1},{17,25},{25,17},{2,10},{10... | collective-permute-start | bytes 380936 | tf_op jit(solution)/shard_map/ppermute | solution.py:457
  67.4 10.3 %collective-permute-start.5 = (bf16[496,128]{1,0:T(8,128)(2,1)S(1)}, bf16[496,128]{1,0:T(8,128)(2,1)S(1)}, u32[]{:S(2)}, u32[]{:S(2)}) collective-permute-start(bf16[496,128]{1,0:T(8,128)(2,1)S(1)} %get-tuple-element.56), channel_id=1, source_target_pairs={{0,16},{8,24},{16,0},{24,8},{1,17},{9,25},{17,1},{25,9},{2,18},{10... | collective-permute-start | bytes 380936 | tf_op jit(solution)/shard_map/ppermute | solution.py:457
  69.0 8.7 %collective-permute-start.6 = (bf16[496,128]{1,0:T(8,128)(2,1)S(1)}, bf16[496,128]{1,0:T(8,128)(2,1)S(1)}, u32[]{:S(2)}, u32[]{:S(2)}) collective-permute-start(bf16[496,128]{1,0:T(8,128)(2,1)S(1)} %get-tuple-element.57), channel_id=1, source_target_pairs={{0,24},{8,16},{16,8},{24,0},{1,25},{9,17},{17,9},{25,1},{2,26},{10... | collective-permute-start | bytes 380936 | tf_op jit(solution)/shard_map/ppermute | solution.py:457
  82.9 9.0 %collective-permute-start.9 = (bf16[960,128]{1,0:T(8,128)(2,1)S(1)}, bf16[960,128]{1,0:T(8,128)(2,1)S(1)}, u32[]{:S(2)}, u32[]{:S(2)}) collective-permute-start(bf16[960,128]{1,0:T(8,128)(2,1)S(1)} %tail.3.refs_0_), channel_id=1, source_target_pairs={{0,6},{2,4},{4,2},{6,0},{1,7},{3,5},{5,3},{7,1},{8,14},{10,12},{12... | collective-permute-start | bytes 737288 | tf_op jit(solution)/shard_map/ppermute | solution.py:457
  83.9 8.0 %collective-permute-start.8 = (bf16[960,128]{1,0:T(8,128)(2,1)S(1)}, bf16[960,128]{1,0:T(8,128)(2,1)S(1)}, u32[]{:S(2)}, u32[]{:S(2)}) collective-permute-start(bf16[960,128]{1,0:T(8,128)(2,1)S(1)} %tail.3.refs_0_), channel_id=1, source_target_pairs={{0,4},{2,6},{4,0},{6,2},{1,5},{3,7},{5,1},{7,3},{8,12},{10,14},{12... | collective-permute-start | bytes 737288 | tf_op jit(solution)/shard_map/ppermute | solution.py:457
  86.4 6.1 %collective-permute-start.7 = (bf16[960,128]{1,0:T(8,128)(2,1)S(1)}, bf16[960,128]{1,0:T(8,128)(2,1)S(1)}, u32[]{:S(2)}, u32[]{:S(2)}) collective-permute-start(bf16[960,128]{1,0:T(8,128)(2,1)S(1)} %tail.3.refs_0_), channel_id=1, source_target_pairs={{0,2},{2,0},{4,6},{6,4},{1,3},{3,1},{5,7},{7,5},{8,10},{10,8},{12,... | collective-permute-start | bytes 737288 | tf_op jit(solution)/shard_map/ppermute | solution.py:457
  97.7 7.1 %collective-permute-start.11 = (bf16[256,128]{1,0:T(8,128)(2,1)S(1)}, bf16[256,128]{1,0:T(8,128)(2,1)S(1)}, u32[]{:S(2)}, u32[]{:S(2)}) collective-permute-start(bf16[256,128]{1,0:T(8,128)(2,1)S(1)} %get-tuple-element.61), channel_id=1, source_target_pairs={{0,16},{8,24},{16,0},{24,8},{1,17},{9,25},{17,1},{25,9},{2,18},{10... | collective-permute-start | bytes 196616 | tf_op jit(solution)/shard_map/ppermute | solution.py:457
  127.0 10.7 %all-to-all-start.4 = ((bf16[8,32,128]{2,1,0:T(8,128)(2,1)}), bf16[8,32,128]{2,1,0:T(8,128)(2,1)S(1)}, u32[]{:S(2)}, u32[]{:S(2)}) async-start(bf16[8,32,128]{2,1,0:T(8,128)(2,1)} %summed.4), calls=%async_computation.4 | async-start | bytes 131072 | tf_op jit(solution)/shard_map/all_to_all | solution.py:451
  137.7 10.4 %collective-permute-start.13 = (bf16[496,128]{1,0:T(8,128)(2,1)S(1)}, bf16[496,128]{1,0:T(8,128)(2,1)S(1)}, u32[]{:S(2)}, u32[]{:S(2)}) collective-permute-start(bf16[496,128]{1,0:T(8,128)(2,1)S(1)} %get-tuple-element.65), channel_id=1, source_target_pairs={{0,8},{8,0},{16,24},{24,16},{1,9},{9,1},{17,25},{25,17},{2,10},{10... | collective-permute-start | bytes 380936 | tf_op jit(solution)/shard_map/ppermute | solution.py:457
  137.8 10.3 %collective-permute-start.14 = (bf16[496,128]{1,0:T(8,128)(2,1)S(1)}, bf16[496,128]{1,0:T(8,128)(2,1)S(1)}, u32[]{:S(2)}, u32[]{:S(2)}) collective-permute-start(bf16[496,128]{1,0:T(8,128)(2,1)S(1)} %get-tuple-element.66), channel_id=1, source_target_pairs={{0,16},{8,24},{16,0},{24,8},{1,17},{9,25},{17,1},{25,9},{2,18},{10... | collective-permute-start | bytes 380936 | tf_op jit(solution)/shard_map/ppermute | solution.py:457
  139.3 8.8 %collective-permute-start.15 = (bf16[496,128]{1,0:T(8,128)(2,1)S(1)}, bf16[496,128]{1,0:T(8,128)(2,1)S(1)}, u32[]{:S(2)}, u32[]{:S(2)}) collective-permute-start(bf16[496,128]{1,0:T(8,128)(2,1)S(1)} %get-tuple-element.67), channel_id=1, source_target_pairs={{0,24},{8,16},{16,8},{24,0},{1,25},{9,17},{17,9},{25,1},{2,26},{10... | collective-permute-start | bytes 380936 | tf_op jit(solution)/shard_map/ppermute | solution.py:457
  153.3 9.0 %collective-permute-start.18 = (bf16[960,128]{1,0:T(8,128)(2,1)S(1)}, bf16[960,128]{1,0:T(8,128)(2,1)S(1)}, u32[]{:S(2)}, u32[]{:S(2)}) collective-permute-start(bf16[960,128]{1,0:T(8,128)(2,1)S(1)} %tail.4.refs_0_), channel_id=1, source_target_pairs={{0,6},{2,4},{4,2},{6,0},{1,7},{3,5},{5,3},{7,1},{8,14},{10,12},{12... | collective-permute-start | bytes 737288 | tf_op jit(solution)/shard_map/ppermute | solution.py:457
  155.1 7.2 %collective-permute-start.17 = (bf16[960,128]{1,0:T(8,128)(2,1)S(1)}, bf16[960,128]{1,0:T(8,128)(2,1)S(1)}, u32[]{:S(2)}, u32[]{:S(2)}) collective-permute-start(bf16[960,128]{1,0:T(8,128)(2,1)S(1)} %tail.4.refs_0_), channel_id=1, source_target_pairs={{0,4},{2,6},{4,0},{6,2},{1,5},{3,7},{5,1},{7,3},{8,12},{10,14},{12... | collective-permute-start | bytes 737288 | tf_op jit(solution)/shard_map/ppermute | solution.py:457
  190.1 11.8 %all-to-all-start.6 = ((bf16[8,32,128]{2,1,0:T(8,128)(2,1)}), bf16[8,32,128]{2,1,0:T(8,128)(2,1)S(1)}, u32[]{:S(2)}, u32[]{:S(2)}) async-start(bf16[8,32,128]{2,1,0:T(8,128)(2,1)} %summed.5), calls=%async_computation.6 | async-start | bytes 131072 | tf_op jit(solution)/shard_map/all_to_all | solution.py:451
  201.9 10.4 %collective-permute-start.22 = (bf16[496,128]{1,0:T(8,128)(2,1)S(1)}, bf16[496,128]{1,0:T(8,128)(2,1)S(1)}, u32[]{:S(2)}, u32[]{:S(2)}) collective-permute-start(bf16[496,128]{1,0:T(8,128)(2,1)S(1)} %get-tuple-element.75), channel_id=1, source_target_pairs={{0,8},{8,0},{16,24},{24,16},{1,9},{9,1},{17,25},{25,17},{2,10},{10... | collective-permute-start | bytes 380936 | tf_op jit(solution)/shard_map/ppermute | solution.py:457
  202.0 10.3 %collective-permute-start.23 = (bf16[496,128]{1,0:T(8,128)(2,1)S(1)}, bf16[496,128]{1,0:T(8,128)(2,1)S(1)}, u32[]{:S(2)}, u32[]{:S(2)}) collective-permute-start(bf16[496,128]{1,0:T(8,128)(2,1)S(1)} %get-tuple-element.76), channel_id=1, source_target_pairs={{0,16},{8,24},{16,0},{24,8},{1,17},{9,25},{17,1},{25,9},{2,18},{10... | collective-permute-start | bytes 380936 | tf_op jit(solution)/shard_map/ppermute | solution.py:457
  204.7 7.6 %collective-permute-start.24 = (bf16[496,128]{1,0:T(8,128)(2,1)S(1)}, bf16[496,128]{1,0:T(8,128)(2,1)S(1)}, u32[]{:S(2)}, u32[]{:S(2)}) collective-permute-start(bf16[496,128]{1,0:T(8,128)(2,1)S(1)} %get-tuple-element.77), channel_id=1, source_target_pairs={{0,24},{8,16},{16,8},{24,0},{1,25},{9,17},{17,9},{25,1},{2,26},{10... | collective-permute-start | bytes 380936 | tf_op jit(solution)/shard_map/ppermute | solution.py:457
  217.5 9.0 %collective-permute-start.27 = (bf16[960,128]{1,0:T(8,128)(2,1)S(1)}, bf16[960,128]{1,0:T(8,128)(2,1)S(1)}, u32[]{:S(2)}, u32[]{:S(2)}) collective-permute-start(bf16[960,128]{1,0:T(8,128)(2,1)S(1)} %tail.5.refs_0_), channel_id=1, source_target_pairs={{0,6},{2,4},{4,2},{6,0},{1,7},{3,5},{5,3},{7,1},{8,14},{10,12},{12... | collective-permute-start | bytes 737288 | tf_op jit(solution)/shard_map/ppermute | solution.py:457
  219.5 7.0 %collective-permute-start.26 = (bf16[960,128]{1,0:T(8,128)(2,1)S(1)}, bf16[960,128]{1,0:T(8,128)(2,1)S(1)}, u32[]{:S(2)}, u32[]{:S(2)}) collective-permute-start(bf16[960,128]{1,0:T(8,128)(2,1)S(1)} %tail.5.refs_0_), channel_id=1, source_target_pairs={{0,4},{2,6},{4,0},{6,2},{1,5},{3,7},{5,1},{7,3},{8,12},{10,14},{12... | collective-permute-start | bytes 737288 | tf_op jit(solution)/shard_map/ppermute | solution.py:457
  228.6 16.9 %collective-permute-start.28 = (f32[960,128]{1,0:T(8,128)S(1)}, f32[960,128]{1,0:T(8,128)S(1)}, u32[]{:S(2)}, u32[]{:S(2)}) collective-permute-start(f32[960,128]{1,0:T(8,128)S(1)} %last.1.mine_ref), channel_id=1, source_target_pairs={{0,1},{1,0},{2,3},{3,2},{4,5},{5,4},{6,7},{7,6},{8,9},{9,8},{10,11... | collective-permute-start | bytes 1474568 | tf_op jit(solution)/shard_map/ppermute | solution.py:587
  (29 other events, 464.8 us)

commit v2 on v1

--- a/solution.py
+++ b/solution.py
@@ -183,7 +183,7 @@
 
 def prepare(source_ref, vir_ref, act_ref, pair_ref, start_ref, inv_ref, act):
     core = lax.axis_index("c")
-    avir = source_ref.shape[1]
+    avir = source_ref.shape[0]
     low = start_ref.shape[0] // act
     spare = 2 * low - avir
     at = lane((low, LANES))
@@ -202,7 +202,7 @@
         sides = []
         for part in range(2):
             where = pl.ds(pl.multiple_of(pair * LANES, LANES), LANES)
-            values = source_ref[part, :, where]
+            values = source_ref[:, part, where]
             values = jnp.where(core == 0, values, pltpu.roll(values, LANES - 32, 1))
             sides += lifted(values, 0.0)
         order = (sides[0], sides[2], sides[1], sides[3])
@@ -291,7 +291,7 @@
 
 def output_kernel(act, mine_ref, theirs_ref, out_ref):
     core = lax.axis_index("c")
-    avir = out_ref.shape[1]
+    avir = out_ref.shape[0]
     low = mine_ref.shape[0] // act
     at = lane((low, LANES))
 
@@ -312,7 +312,7 @@
                     value = moved if value is None else jnp.where(at < 32 * (n + 1), moved, value)
                 rows = low if side == 0 else avir - low
                 where = pl.ds(pl.multiple_of(pair * LANES, LANES), LANES)
-                out_ref[part, pl.ds(side * low, rows), where] = value[:rows]
+                out_ref[pl.ds(side * low, rows), part, where] = value[:rows]
 
 
 def total_of(refs, at, rows):
@@ -564,27 +564,29 @@
     )
     output = call(
         functools.partial(output_kernel, act),
-        jax.ShapeDtypeStruct((2, avir, act * pairs), F32), [VMEM] * 2, (), "output",
+        jax.ShapeDtypeStruct((avir, 2, act * pairs), F32), [VMEM] * 2, (), "output",
     )
 
     for step in range(PASSES):
         if step == 0:
             start, inverse, share_now, part = opening(
-                source, eps_vir.reshape(avir, 1), eps_act, energy, own
+                source.transpose(1, 0, 2), eps_vir.reshape(avir, 1), eps_act, energy, own
             )
             state = start
             part = second(start, part, other)
-            part, couple = lax.optimization_barrier((part, couple))
-            couple = laid_out(couple, low, ny)
         else:
             state, share_now, *part = later(*recv, state, kron, start, inverse, blocks)
-        mixed = exchange(along_z(*swapped(part, "y"), share_now), "z")
+        mixed = along_z(*swapped(part, "y"), share_now)
+        if step == 0:
+            mixed, couple = lax.optimization_barrier((mixed, couple))
+            couple = laid_out(couple, low, ny)
+        mixed = exchange(mixed, "z")
         inter = exchange(summed(mixed), "z")
         mixed = along_y(inter, coupled(mixed, couple))
         blocks = stage(mixed[0], own, other)
         recv = swapped([tail(*swapped(mixed, "y"), blocks)] * nx, "x")
     state = last(*recv, state, kron, start, inverse)
-    return output(state, lax.ppermute(state, "c", swap))
+    return output(state, lax.ppermute(state, "c", swap)).transpose(1, 0, 2)
 
 
 def solution(mesh, sizes=(8, 4, 4, 2)):

time: 249 us -> 250 us (level)
  waiting for transfers between devices: 54.1 us -> 56.6 us
    ppermute x27, waiting for transfers between devices: 26.7 us -> 31.2 us  [swapped(): lax.ppermute(values[k], axis, [(i, i ^ k) for i in range(size)])]
    unnamed x39 -> x38, local copies, waits for them, and re-layouts: 11.6 us -> 11.4 us
  transfers between devices with their start and end apart: 34 -> 34, of which waited for: 18 -> 19; matrix products, arithmetic and copies ran while one was open for 4% -> 4% of each run, Pallas kernels for 10% -> 11%
where the time goes in v2:
time: 250 us; the launch traced here: 249 us
  starting transfers between devices  79.4 us (32%)
  Pallas kernels  57.2 us (23%)
  waiting for transfers between devices  56.6 us (23%)
  blocking collectives  34 us (14%)
  local copies, waits for them, and re-layouts  21.4 us (9%)
    ppermute x27, starting transfers between devices, swapped(): lax.ppermute(values[k], axis, [(i, i ^ k) for i in range(size)])  37.9 us
    all_to_all x2, blocking collectives, exchange(): return lax.all_to_all(copies, axis, 0, 0, tiled=True)  34 us
    ppermute x27, waiting for transfers between devices, swapped(): lax.ppermute(values[k], axis, [(i, i ^ k) for i in range(size)])  31.2 us
    all_to_all x5, starting transfers between devices, exchange(): return lax.all_to_all(copies, axis, 0, 0, tiled=True)  24.1 us
    all_to_all x5, waiting for transfers between devices, exchange(): return lax.all_to_all(copies, axis, 0, 0, tiled=True)  24 us
    pallas_call x3, Pallas kernels, per_device(): recv = swapped([tail(*swapped(mixed, 'y'), blocks)] * nx, 'x')  15.5 us
    ppermute x1, starting transfers between devices, per_device(): return output(state, lax.ppermute(state, 'c', swap)).transpose(1, 0, 2)  14 us
    unnamed x38, local copies, waits for them, and re-layouts  11.4 us
  transfers between devices with their start and end apart: 34, of which 19 were waited for; matrix products, arithmetic and copies ran while one was open for 4% of the time, Pallas kernels for 11%

profile of v2, /device:TPU:1, one launch (start us, length us, event | category | flops | bytes accessed | tf_op | source)
XLA Modules:
  0.0 249.1 jit_solution(5839500982509765671)
XLA Ops:
  5.0 5.8 %all-to-all-start = ((bf16[8,2,75,300]{3,1,2,0:T(2,128)(2,1)}), bf16[8,2,75,300]{3,1,2,0:T(2,128)(2,1)}, u32[]{:S(2)}, u32[]{:S(2)}) async-start(bf16[8,2,75,300]{3,1,2,0:T(2,128)(2,1)} %broadcast_in_dim.2), calls=%async_computation | async-start | bytes 1843200 | tf_op jit(solution)/shard_map/all_to_all | solution.py:451
  13.9 5.3 %opening.1 = (f32[960,128]{1,0:T(8,128)S(1)}, f32[960,128]{1,0:T(8,128)S(1)}, bf16[240,128]{1,0:T(8,128)(2,1)S(1)}, bf16[2,256,128]{2,1,0:T(8,128)(2,1)S(1)}) custom-call(f32[75,2,1536]{2,1,0:T(2,128)S(1)} %bitcast.14, f32[75,1]{1,0:T(8,128)S(1)} %copy.10.vir_ref, f32[24]{0:T(128)S(1)} %copy-done.16, f32[1,128]{1,0:T(1,128)S(1)} %reshape_tile.3.pair_ref, ...), custom_call_target="tpu_custom_call" | custom-call | flops 412876800 | bytes 6451200 | tf_op jit(solution)/shard_map/opening/pallas_call | solution.py:572
  19.3 3.7 %second.1 = (bf16[256,128]{1,0:T(8,128)(2,1)S(1)}, bf16[256,128]{1,0:T(8,128)(2,1)S(1)}, bf16[256,128]{1,0:T(8,128)(2,1)S(1)}, bf16[256,128]{1,0:T(8,128)(2,1)S(1)}) custom-call(f32[960,128]{1,0:T(8,128)S(1)} %get-tuple-element.39.start_ref.refs_4_.refs_6_, bf16[2,256,128]{2,1,0:T(8,128)(2,1)S(1)} %get-tuple-element.40.first_ref, ...), custom_call_target="tpu_custom_call" | custom-call | flops 412876800 | bytes 6451200 | tf_op jit(solution)/shard_map/second/pallas_call | solution.py:576
  30.8 8.2 %all-to-all-start.1 = ((bf16[8,272,128]{2,1,0:T(8,128)(2,1)}), bf16[8,272,128]{2,1,0:T(8,128)(2,1)S(1)}, u32[]{:S(2)}, u32[]{:S(2)}) async-start(bf16[8,272,128]{2,1,0:T(8,128)(2,1)} %along_z.3), calls=%async_computation.1 | async-start | bytes 1114112 | tf_op jit(solution)/shard_map/all_to_all | solution.py:451
  42.3 13.2 %all-to-all-done.1.recv_ref = bf16[8,272,128]{2,1,0:T(8,128)(2,1)S(1)} async-done(((bf16[8,272,128]{2,1,0:T(8,128)(2,1)}), bf16[8,272,128]{2,1,0:T(8,128)(2,1)S(1)}, u32[]{:S(2)}, u32[]{:S(2)}) %all-to-all-start.1) | async-done | bytes 557088 | tf_op jit(solution)/shard_map/all_to_all | solution.py:451
  74.7 3.6 %stage.3.refs_4_.refs_8_ = bf16[2,2,1984,896]{3,2,1,0:T(8,128)(2,1)S(1)} custom-call(bf16[496,128]{1,0:T(8,128)(2,1)S(1)} %get-tuple-element.48.after.refs_0_, bf16[2,1800,896]{2,1,0:T(8,128)(2,1)S(1)} %bitcast.11, bf16[2,1800,896]{2,1,0:T(8,128)(2,1)} %collective-permute-done.other), custom_call_target="tpu_custom_call" | custom-call | bytes 51609600 | tf_op jit(solution)/shard_map/stage/pallas_call | solution.py:586
  78.9 5.1 %tail.3.refs_0_ = bf16[960,128]{1,0:T(8,128)(2,1)S(1)} custom-call(bf16[496,128]{1,0:T(8,128)(2,1)S(1)} %get-tuple-element.48.after.refs_0_, bf16[496,128]{1,0:T(8,128)(2,1)S(1)} %collective-permute-done.4.refs_1_, bf16[496,128]{1,0:T(8,128)(2,1)S(1)} %collective-permute-done.5.refs_2_, bf16[496,128]{1,0:T(8,128)(2,1)S(1)} %collective-permute-done.6.refs_3_, ...), custom_call_target="tpu_custom_call" | custom-call | flops 825753600 | bytes 3225600 | tf_op jit(solution)/shard_map/tail/pallas_call | solution.py:587
  87.9 7.9 %collective-permute-done.9.refs_3_ = bf16[960,128]{1,0:T(8,128)(2,1)S(1)} collective-permute-done((bf16[960,128]{1,0:T(8,128)(2,1)S(1)}, bf16[960,128]{1,0:T(8,128)(2,1)S(1)}, u32[]{:S(2)}, u32[]{:S(2)}) %collective-permute-start.9) | collective-permute-done | bytes 245792 | tf_op jit(solution)/shard_map/ppermute | solution.py:457
  95.8 4.5 %later.2 = (f32[960,128]{1,0:T(8,128)S(1)}, bf16[240,128]{1,0:T(8,128)(2,1)S(1)}, bf16[256,128]{1,0:T(8,128)(2,1)S(1)}, bf16[256,128]{1,0:T(8,128)(2,1)S(1)}, bf...) custom-call(bf16[960,128]{1,0:T(8,128)(2,1)S(1)} %tail.3.refs_0_, ...), custom_call_target="tpu_custom_call" | custom-call | flops 825753600 | bytes 3225600 | tf_op jit(solution)/shard_map/later/pallas_call | solution.py:578
  100.4 3.6 %collective-permute-start.11 = (bf16[256,128]{1,0:T(8,128)(2,1)S(1)}, bf16[256,128]{1,0:T(8,128)(2,1)S(1)}, u32[]{:S(2)}, u32[]{:S(2)}) collective-permute-start(bf16[256,128]{1,0:T(8,128)(2,1)S(1)} %get-tuple-element.55), channel_id=1, source_target_pairs={{0,16},{8,24},{16,0},{24,8},{1,17},{9,25},{17,1},{25,9},{2,18},{10... | collective-permute-start | bytes 196616 | tf_op jit(solution)/shard_map/ppermute | solution.py:457
  108.5 19.1 %all_to_all.35.recv_ref = bf16[8,272,128]{2,1,0:T(8,128)(2,1)S(1)} all-to-all(bf16[8,272,128]{2,1,0:T(8,128)(2,1)S(1)} %along_z.4), channel_id=1, replica_groups=mesh['z'=8,'y'=4,'x'=4,'c'=2] {'z'}, dimensions={0} | all-to-all | bytes 1114112 | tf_op jit(solution)/shard_map/all_to_all | solution.py:451
  128.2 3.4 %all-to-all-start.4 = ((bf16[8,32,128]{2,1,0:T(8,128)(2,1)}), bf16[8,32,128]{2,1,0:T(8,128)(2,1)S(1)}, u32[]{:S(2)}, u32[]{:S(2)}) async-start(bf16[8,32,128]{2,1,0:T(8,128)(2,1)} %summed.4), calls=%async_computation.4 | async-start | bytes 131072 | tf_op jit(solution)/shard_map/all_to_all | solution.py:451
  133.7 5.2 %all-to-all-done.4.inter_ref = bf16[8,32,128]{2,1,0:T(8,128)(2,1)S(1)} async-done(((bf16[8,32,128]{2,1,0:T(8,128)(2,1)}), bf16[8,32,128]{2,1,0:T(8,128)(2,1)S(1)}, u32[]{:S(2)}, u32[]{:S(2)}) %all-to-all-start.4) | async-done | bytes 65568 | tf_op jit(solution)/shard_map/all_to_all | solution.py:451
  146.8 3.6 %stage.4.refs_4_.refs_8_ = bf16[2,2,1984,896]{3,2,1,0:T(8,128)(2,1)S(1)} custom-call(bf16[496,128]{1,0:T(8,128)(2,1)S(1)} %get-tuple-element.58.after.refs_0_, bf16[2,1800,896]{2,1,0:T(8,128)(2,1)S(1)} %bitcast.12, bf16[2,1800,896]{2,1,0:T(8,128)(2,1)} %collective-permute-done.other), custom_call_target="tpu_custom_call" | custom-call | bytes 51609600 | tf_op jit(solution)/shard_map/stage/pallas_call | solution.py:586
  150.4 5.2 %tail.4.refs_0_ = bf16[960,128]{1,0:T(8,128)(2,1)S(1)} custom-call(bf16[496,128]{1,0:T(8,128)(2,1)S(1)} %get-tuple-element.58.after.refs_0_, bf16[496,128]{1,0:T(8,128)(2,1)S(1)} %collective-permute-done.13.refs_1_, bf16[496,128]{1,0:T(8,128)(2,1)S(1)} %collective-permute-done.14.refs_2_, bf16[496,128]{1,0:T(8,128)(2,1)S(1)} %collective-permute-done.15.refs_3_, ...), custom_call_target="tpu_custom_call" | custom-call | flops 825753600 | bytes 3225600 | tf_op jit(solution)/shard_map/tail/pallas_call | solution.py:587
  155.6 4.7 %collective-permute-start.18 = (bf16[960,128]{1,0:T(8,128)(2,1)S(1)}, bf16[960,128]{1,0:T(8,128)(2,1)S(1)}, u32[]{:S(2)}, u32[]{:S(2)}) collective-permute-start(bf16[960,128]{1,0:T(8,128)(2,1)S(1)} %tail.4.refs_0_), channel_id=1, source_target_pairs={{0,6},{2,4},{4,2},{6,0},{1,7},{3,5},{5,3},{7,1},{8,14},{10,12},{12... | collective-permute-start | bytes 737288 | tf_op jit(solution)/shard_map/ppermute | solution.py:457
  161.0 5.1 %collective-permute-done.18.refs_3_ = bf16[960,128]{1,0:T(8,128)(2,1)S(1)} collective-permute-done((bf16[960,128]{1,0:T(8,128)(2,1)S(1)}, bf16[960,128]{1,0:T(8,128)(2,1)S(1)}, u32[]{:S(2)}, u32[]{:S(2)}) %collective-permute-start.18) | collective-permute-done | bytes 245792 | tf_op jit(solution)/shard_map/ppermute | solution.py:457
  167.2 4.5 %later.3 = (f32[960,128]{1,0:T(8,128)S(1)}, bf16[240,128]{1,0:T(8,128)(2,1)S(1)}, bf16[256,128]{1,0:T(8,128)(2,1)S(1)}, bf16[256,128]{1,0:T(8,128)(2,1)S(1)}, bf...) custom-call(bf16[960,128]{1,0:T(8,128)(2,1)S(1)} %tail.4.refs_0_, ...), custom_call_target="tpu_custom_call" | custom-call | flops 825753600 | bytes 3225600 | tf_op jit(solution)/shard_map/later/pallas_call | solution.py:578
  178.8 14.9 %all_to_all.36.recv_ref = bf16[8,272,128]{2,1,0:T(8,128)(2,1)S(1)} all-to-all(bf16[8,272,128]{2,1,0:T(8,128)(2,1)S(1)} %along_z.5), channel_id=1, replica_groups=mesh['z'=8,'y'=4,'x'=4,'c'=2] {'z'}, dimensions={0} | all-to-all | bytes 1114112 | tf_op jit(solution)/shard_map/all_to_all | solution.py:451
  199.7 5.2 %all-to-all-done.6.inter_ref = bf16[8,32,128]{2,1,0:T(8,128)(2,1)S(1)} async-done(((bf16[8,32,128]{2,1,0:T(8,128)(2,1)}), bf16[8,32,128]{2,1,0:T(8,128)(2,1)S(1)}, u32[]{:S(2)}, u32[]{:S(2)}) %all-to-all-start.6) | async-done | bytes 65568 | tf_op jit(solution)/shard_map/all_to_all | solution.py:451
  211.7 3.6 %stage.5.refs_4_ = bf16[2,2,1984,896]{3,2,1,0:T(8,128)(2,1)S(1)} custom-call(bf16[496,128]{1,0:T(8,128)(2,1)S(1)} %get-tuple-element.68.after.refs_0_, bf16[2,1800,896]{2,1,0:T(8,128)(2,1)S(1)} %bitcast.13, bf16[2,1800,896]{2,1,0:T(8,128)(2,1)} %collective-permute-done.other), custom_call_target="tpu_custom_call" | custom-call | bytes 51609600 | tf_op jit(solution)/shard_map/stage/pallas_call | solution.py:586
  215.3 5.2 %tail.5.refs_0_ = bf16[960,128]{1,0:T(8,128)(2,1)S(1)} custom-call(bf16[496,128]{1,0:T(8,128)(2,1)S(1)} %get-tuple-element.68.after.refs_0_, bf16[496,128]{1,0:T(8,128)(2,1)S(1)} %collective-permute-done.22.refs_1_, bf16[496,128]{1,0:T(8,128)(2,1)S(1)} %collective-permute-done.23.refs_2_, bf16[496,128]{1,0:T(8,128)(2,1)S(1)} %collective-permute-done.24.refs_3_, ...), custom_call_target="tpu_custom_call" | custom-call | flops 825753600 | bytes 3225600 | tf_op jit(solution)/shard_map/tail/pallas_call | solution.py:587
  223.8 5.0 %collective-permute-done.27.refs_3_ = bf16[960,128]{1,0:T(8,128)(2,1)S(1)} collective-permute-done((bf16[960,128]{1,0:T(8,128)(2,1)S(1)}, bf16[960,128]{1,0:T(8,128)(2,1)S(1)}, u32[]{:S(2)}, u32[]{:S(2)}) %collective-permute-start.27) | collective-permute-done | bytes 245792 | tf_op jit(solution)/shard_map/ppermute | solution.py:457
  231.5 14.0 %collective-permute-start.28 = (f32[960,128]{1,0:T(8,128)S(1)}, f32[960,128]{1,0:T(8,128)S(1)}, u32[]{:S(2)}, u32[]{:S(2)}) collective-permute-start(f32[960,128]{1,0:T(8,128)S(1)} %last.1.mine_ref), channel_id=1, source_target_pairs={{0,1},{1,0},{2,3},{3,2},{4,5},{5,4},{6,7},{7,6},{8,9},{9,8},{10,11... | collective-permute-start | bytes 1474568 | tf_op jit(solution)/shard_map/ppermute | solution.py:589
  (118 shorter events, 89.2 us)
Async XLA Ops:
  0.0 19.2 %collective-permute-start = (bf16[2,1800,896]{2,1,0:T(8,128)(2,1)}, bf16[2,1800,896]{2,1,0:T(8,128)(2,1)}, u32[]{:S(2)}, u32[]{:S(2)}) collective-permute-start(bf16[2,1800,896]{2,1,0:T(8,128)(2,1)} %bitcast.9), channel_id=1, source_target_pairs={{0,1},{1,0},{2,3},{3,2},{4,5},{5,4},{6,7},{7,6},{8,9},{9,8},{10,11... | collective-permute-start | bytes 19353608 | tf_op jit(solution)/shard_map/ppermute | solution.py:481
  5.0 25.8 %all-to-all-start = ((bf16[8,2,75,300]{3,1,2,0:T(2,128)(2,1)}), bf16[8,2,75,300]{3,1,2,0:T(2,128)(2,1)}, u32[]{:S(2)}, u32[]{:S(2)}) async-start(bf16[8,2,75,300]{3,1,2,0:T(2,128)(2,1)} %broadcast_in_dim.2), calls=%async_computation | async-start | bytes 1843200 | tf_op jit(solution)/shard_map/all_to_all | solution.py:451
  30.8 24.8 %all-to-all-start.1 = ((bf16[8,272,128]{2,1,0:T(8,128)(2,1)}), bf16[8,272,128]{2,1,0:T(8,128)(2,1)S(1)}, u32[]{:S(2)}, u32[]{:S(2)}) async-start(bf16[8,272,128]{2,1,0:T(8,128)(2,1)} %along_z.3), calls=%async_computation.1 | async-start | bytes 1114112 | tf_op jit(solution)/shard_map/all_to_all | solution.py:451
  56.2 10.5 %all-to-all-start.2 = ((bf16[8,32,128]{2,1,0:T(8,128)(2,1)}), bf16[8,32,128]{2,1,0:T(8,128)(2,1)S(1)}, u32[]{:S(2)}, u32[]{:S(2)}) async-start(bf16[8,32,128]{2,1,0:T(8,128)(2,1)} %summed.3), calls=%async_computation.2 | async-start | bytes 131072 | tf_op jit(solution)/shard_map/all_to_all | solution.py:451
  66.7 11.5 %collective-permute-start.4 = (bf16[496,128]{1,0:T(8,128)(2,1)S(1)}, bf16[496,128]{1,0:T(8,128)(2,1)S(1)}, u32[]{:S(2)}, u32[]{:S(2)}) collective-permute-start(bf16[496,128]{1,0:T(8,128)(2,1)S(1)} %get-tuple-element.49), channel_id=1, source_target_pairs={{0,8},{8,0},{16,24},{24,16},{1,9},{9,1},{17,25},{25,17},{2,10},{10... | collective-permute-start | bytes 380936 | tf_op jit(solution)/shard_map/ppermute | solution.py:457
  69.3 8.9 %collective-permute-start.5 = (bf16[496,128]{1,0:T(8,128)(2,1)S(1)}, bf16[496,128]{1,0:T(8,128)(2,1)S(1)}, u32[]{:S(2)}, u32[]{:S(2)}) collective-permute-start(bf16[496,128]{1,0:T(8,128)(2,1)S(1)} %get-tuple-element.50), channel_id=1, source_target_pairs={{0,16},{8,24},{16,0},{24,8},{1,17},{9,25},{17,1},{25,9},{2,18},{10... | collective-permute-start | bytes 380936 | tf_op jit(solution)/shard_map/ppermute | solution.py:457
  71.8 7.0 %collective-permute-start.6 = (bf16[496,128]{1,0:T(8,128)(2,1)S(1)}, bf16[496,128]{1,0:T(8,128)(2,1)S(1)}, u32[]{:S(2)}, u32[]{:S(2)}) collective-permute-start(bf16[496,128]{1,0:T(8,128)(2,1)S(1)} %get-tuple-element.51), channel_id=1, source_target_pairs={{0,24},{8,16},{16,8},{24,0},{1,25},{9,17},{17,9},{25,1},{2,26},{10... | collective-permute-start | bytes 380936 | tf_op jit(solution)/shard_map/ppermute | solution.py:457
  84.0 11.8 %collective-permute-start.9 = (bf16[960,128]{1,0:T(8,128)(2,1)S(1)}, bf16[960,128]{1,0:T(8,128)(2,1)S(1)}, u32[]{:S(2)}, u32[]{:S(2)}) collective-permute-start(bf16[960,128]{1,0:T(8,128)(2,1)S(1)} %tail.3.refs_0_), channel_id=1, source_target_pairs={{0,6},{2,4},{4,2},{6,0},{1,7},{3,5},{5,3},{7,1},{8,14},{10,12},{12... | collective-permute-start | bytes 737288 | tf_op jit(solution)/shard_map/ppermute | solution.py:457
  86.2 9.6 %collective-permute-start.8 = (bf16[960,128]{1,0:T(8,128)(2,1)S(1)}, bf16[960,128]{1,0:T(8,128)(2,1)S(1)}, u32[]{:S(2)}, u32[]{:S(2)}) collective-permute-start(bf16[960,128]{1,0:T(8,128)(2,1)S(1)} %tail.3.refs_0_), channel_id=1, source_target_pairs={{0,4},{2,6},{4,0},{6,2},{1,5},{3,7},{5,1},{7,3},{8,12},{10,14},{12... | collective-permute-start | bytes 737288 | tf_op jit(solution)/shard_map/ppermute | solution.py:457
  86.8 9.1 %collective-permute-start.7 = (bf16[960,128]{1,0:T(8,128)(2,1)S(1)}, bf16[960,128]{1,0:T(8,128)(2,1)S(1)}, u32[]{:S(2)}, u32[]{:S(2)}) collective-permute-start(bf16[960,128]{1,0:T(8,128)(2,1)S(1)} %tail.3.refs_0_), channel_id=1, source_target_pairs={{0,2},{2,0},{4,6},{6,4},{1,3},{3,1},{5,7},{7,5},{8,10},{10,8},{12,... | collective-permute-start | bytes 737288 | tf_op jit(solution)/shard_map/ppermute | solution.py:457
  128.2 10.7 %all-to-all-start.4 = ((bf16[8,32,128]{2,1,0:T(8,128)(2,1)}), bf16[8,32,128]{2,1,0:T(8,128)(2,1)S(1)}, u32[]{:S(2)}, u32[]{:S(2)}) async-start(bf16[8,32,128]{2,1,0:T(8,128)(2,1)} %summed.4), calls=%async_computation.4 | async-start | bytes 131072 | tf_op jit(solution)/shard_map/all_to_all | solution.py:451
  139.0 11.4 %collective-permute-start.13 = (bf16[496,128]{1,0:T(8,128)(2,1)S(1)}, bf16[496,128]{1,0:T(8,128)(2,1)S(1)}, u32[]{:S(2)}, u32[]{:S(2)}) collective-permute-start(bf16[496,128]{1,0:T(8,128)(2,1)S(1)} %get-tuple-element.59), channel_id=1, source_target_pairs={{0,8},{8,0},{16,24},{24,16},{1,9},{9,1},{17,25},{25,17},{2,10},{10... | collective-permute-start | bytes 380936 | tf_op jit(solution)/shard_map/ppermute | solution.py:457
  141.4 8.9 %collective-permute-start.14 = (bf16[496,128]{1,0:T(8,128)(2,1)S(1)}, bf16[496,128]{1,0:T(8,128)(2,1)S(1)}, u32[]{:S(2)}, u32[]{:S(2)}) collective-permute-start(bf16[496,128]{1,0:T(8,128)(2,1)S(1)} %get-tuple-element.60), channel_id=1, source_target_pairs={{0,16},{8,24},{16,0},{24,8},{1,17},{9,25},{17,1},{25,9},{2,18},{10... | collective-permute-start | bytes 380936 | tf_op jit(solution)/shard_map/ppermute | solution.py:457
  142.8 7.6 %collective-permute-start.15 = (bf16[496,128]{1,0:T(8,128)(2,1)S(1)}, bf16[496,128]{1,0:T(8,128)(2,1)S(1)}, u32[]{:S(2)}, u32[]{:S(2)}) collective-permute-start(bf16[496,128]{1,0:T(8,128)(2,1)S(1)} %get-tuple-element.61), channel_id=1, source_target_pairs={{0,24},{8,16},{16,8},{24,0},{1,25},{9,17},{17,9},{25,1},{2,26},{10... | collective-permute-start | bytes 380936 | tf_op jit(solution)/shard_map/ppermute | solution.py:457
  155.6 10.5 %collective-permute-start.18 = (bf16[960,128]{1,0:T(8,128)(2,1)S(1)}, bf16[960,128]{1,0:T(8,128)(2,1)S(1)}, u32[]{:S(2)}, u32[]{:S(2)}) collective-permute-start(bf16[960,128]{1,0:T(8,128)(2,1)S(1)} %tail.4.refs_0_), channel_id=1, source_target_pairs={{0,6},{2,4},{4,2},{6,0},{1,7},{3,5},{5,3},{7,1},{8,14},{10,12},{12... | collective-permute-start | bytes 737288 | tf_op jit(solution)/shard_map/ppermute | solution.py:457
  160.3 6.6 %collective-permute-start.17 = (bf16[960,128]{1,0:T(8,128)(2,1)S(1)}, bf16[960,128]{1,0:T(8,128)(2,1)S(1)}, u32[]{:S(2)}, u32[]{:S(2)}) collective-permute-start(bf16[960,128]{1,0:T(8,128)(2,1)S(1)} %tail.4.refs_0_), channel_id=1, source_target_pairs={{0,4},{2,6},{4,0},{6,2},{1,5},{3,7},{5,1},{7,3},{8,12},{10,14},{12... | collective-permute-start | bytes 737288 | tf_op jit(solution)/shard_map/ppermute | solution.py:457
  160.3 6.9 %collective-permute-start.16 = (bf16[960,128]{1,0:T(8,128)(2,1)S(1)}, bf16[960,128]{1,0:T(8,128)(2,1)S(1)}, u32[]{:S(2)}, u32[]{:S(2)}) collective-permute-start(bf16[960,128]{1,0:T(8,128)(2,1)S(1)} %tail.4.refs_0_), channel_id=1, source_target_pairs={{0,2},{2,0},{4,6},{6,4},{1,3},{3,1},{5,7},{7,5},{8,10},{10,8},{12,... | collective-permute-start | bytes 737288 | tf_op jit(solution)/shard_map/ppermute | solution.py:457
  194.3 10.5 %all-to-all-start.6 = ((bf16[8,32,128]{2,1,0:T(8,128)(2,1)}), bf16[8,32,128]{2,1,0:T(8,128)(2,1)S(1)}, u32[]{:S(2)}, u32[]{:S(2)}) async-start(bf16[8,32,128]{2,1,0:T(8,128)(2,1)} %summed.5), calls=%async_computation.6 | async-start | bytes 131072 | tf_op jit(solution)/shard_map/all_to_all | solution.py:451
  204.9 10.4 %collective-permute-start.22 = (bf16[496,128]{1,0:T(8,128)(2,1)S(1)}, bf16[496,128]{1,0:T(8,128)(2,1)S(1)}, u32[]{:S(2)}, u32[]{:S(2)}) collective-permute-start(bf16[496,128]{1,0:T(8,128)(2,1)S(1)} %get-tuple-element.69), channel_id=1, source_target_pairs={{0,8},{8,0},{16,24},{24,16},{1,9},{9,1},{17,25},{25,17},{2,10},{10... | collective-permute-start | bytes 380936 | tf_op jit(solution)/shard_map/ppermute | solution.py:457
  205.0 10.3 %collective-permute-start.23 = (bf16[496,128]{1,0:T(8,128)(2,1)S(1)}, bf16[496,128]{1,0:T(8,128)(2,1)S(1)}, u32[]{:S(2)}, u32[]{:S(2)}) collective-permute-start(bf16[496,128]{1,0:T(8,128)(2,1)S(1)} %get-tuple-element.70), channel_id=1, source_target_pairs={{0,16},{8,24},{16,0},{24,8},{1,17},{9,25},{17,1},{25,9},{2,18},{10... | collective-permute-start | bytes 380936 | tf_op jit(solution)/shard_map/ppermute | solution.py:457
  207.4 7.8 %collective-permute-start.24 = (bf16[496,128]{1,0:T(8,128)(2,1)S(1)}, bf16[496,128]{1,0:T(8,128)(2,1)S(1)}, u32[]{:S(2)}, u32[]{:S(2)}) collective-permute-start(bf16[496,128]{1,0:T(8,128)(2,1)S(1)} %get-tuple-element.71), channel_id=1, source_target_pairs={{0,24},{8,16},{16,8},{24,0},{1,25},{9,17},{17,9},{25,1},{2,26},{10... | collective-permute-start | bytes 380936 | tf_op jit(solution)/shard_map/ppermute | solution.py:457
  220.5 8.4 %collective-permute-start.27 = (bf16[960,128]{1,0:T(8,128)(2,1)S(1)}, bf16[960,128]{1,0:T(8,128)(2,1)S(1)}, u32[]{:S(2)}, u32[]{:S(2)}) collective-permute-start(bf16[960,128]{1,0:T(8,128)(2,1)S(1)} %tail.5.refs_0_), channel_id=1, source_target_pairs={{0,6},{2,4},{4,2},{6,0},{1,7},{3,5},{5,3},{7,1},{8,14},{10,12},{12... | collective-permute-start | bytes 737288 | tf_op jit(solution)/shard_map/ppermute | solution.py:457
  223.4 6.7 %collective-permute-start.25 = (bf16[960,128]{1,0:T(8,128)(2,1)S(1)}, bf16[960,128]{1,0:T(8,128)(2,1)S(1)}, u32[]{:S(2)}, u32[]{:S(2)}) collective-permute-start(bf16[960,128]{1,0:T(8,128)(2,1)S(1)} %tail.5.refs_0_), channel_id=1, source_target_pairs={{0,2},{2,0},{4,6},{6,4},{1,3},{3,1},{5,7},{7,5},{8,10},{10,8},{12,... | collective-permute-start | bytes 737288 | tf_op jit(solution)/shard_map/ppermute | solution.py:457
  231.5 15.5 %collective-permute-start.28 = (f32[960,128]{1,0:T(8,128)S(1)}, f32[960,128]{1,0:T(8,128)S(1)}, u32[]{:S(2)}, u32[]{:S(2)}) collective-permute-start(f32[960,128]{1,0:T(8,128)S(1)} %last.1.mine_ref), channel_id=1, source_target_pairs={{0,1},{1,0},{2,3},{3,2},{4,5},{5,4},{6,7},{7,6},{8,9},{9,8},{10,11... | collective-permute-start | bytes 1474568 | tf_op jit(solution)/shard_map/ppermute | solution.py:589
  (29 other events, 484.4 us)
